TPU v7x, 256 devices: a whole 4x4x8 slice. The times are simulated.
256 devices in a mesh: theta: 4 (over x), state: 64 (over z, y, core).
Axes of the slice: x: 4, y: 4, z: 8, core: 2. Of those that a mesh axis runs over, the one named last changes fastest.
Arguments:
- states: bfloat16 [32, 32768, 256], P('theta', 'state'), may hold values from -4.875 to 4.875
- log_vol: bfloat16 [32, 32768], P('theta', 'state'), may hold values from -3 to 3
- transition: bfloat16 [32, 256, 256], P('theta'), may hold values from -0.375 to 0.375
- loading: bfloat16 [256, 128], replicated, may hold values from -0.375 to 0.375
- yields: float32 [3, 128], replicated, may hold values from -5 to 5
- state_noise: bfloat16 [3, 32768, 256], P(None, 'state'), may hold values from -5 to 5
- vol_noise: float32 [3, 32768], P(None, 'state'), may hold values from -5 to 5
- vol_mean: float32 [32], replicated, may hold values from -1.5 to 0
- vol_persist: float32 [32], replicated, may hold values from 0.3 to 0.95
- vol_scale: float32 [32], replicated, may hold values from 0.1 to 0.6
- obs_prec: float32 [32], replicated, may hold values from 0.05 to 4
- prior_loglik: float32 [32], replicated, may hold values from -12 to 12
- ancestors: int32 [32], replicated, may hold values from 0 to 31, as said below
- counts: int32 [3, 32, 64], P(None, 'theta', 'state'), may hold values from 256 to 768, as said below
- local_anc: int32 [3, 32, 49152], P(None, 'theta', 'state'), may hold values from 0 to 511
Outputs:
- final_states: bfloat16 [32, 32768, 256], P('theta', 'state')
- final_vol: bfloat16 [32, 32768], P('theta', 'state')
- loglik: float32 [32], P('theta')
Inputs may be any that keep to these rules, and one draw needn't show every extreme that they name: ancestors[i] lies in the group of 8 consecutive indices that holds i or in one of the two groups beside it; at most 4 indices of one group name the group below it and at most 4 name the group above it; both bounds are reached. For each step and parameter particle the counts over the shards sum to 32768; the sum of the counts of shards 0 to j - 1 differs from j * 512 by at most 128, and for each step and particle some shard reaches + 128 and some - 128. `local_anc`: only the first counts[t, i, j] slots of shard j's block are used.
All inputs are finite; a program needn't handle non-finite values.
Results may differ from a plain program's by a relative error of at most 0.001.
The roundings to bfloat16 on the way count: a program that leaves them out, or rounds other values in their place, can miss the bound.
Values may be sent and summed in bfloat16 or wider, within the bound.
A program may use at most 64 MiB of HBM per device.

v0:
```python
import math

import jax
import jax.numpy as jnp
from jax import lax
from jax.sharding import PartitionSpec as P

M = 128
STEPS = 3


def padded(block, sides, width):
    for axis, dim in sides:
        count = lax.axis_size(axis)
        forward = [(i, i + 1) for i in range(count - 1)]
        backward = [(target, source) for source, target in forward]
        low = lax.ppermute(
            lax.slice_in_dim(block, block.shape[dim] - width, None, axis=dim), axis, forward
        )
        high = lax.ppermute(lax.slice_in_dim(block, 0, width, axis=dim), axis, backward)
        block = jnp.concatenate([low, block, high], axis=dim)
    return block


def sent_to_all(x, axis):
    copies = jnp.broadcast_to(x, (lax.axis_size(axis), *x.shape))
    return lax.all_to_all(copies, axis, split_axis=0, concat_axis=0, tiled=True)


def joined_by_halves(pieces, combine):
    while len(jax.tree.leaves(pieces)[0]) > 1:
        pieces = jax.vmap(combine)(
            *(jax.tree.map(lambda part: part[side::2], pieces) for side in (0, 1))
        )
    return jax.tree.map(lambda part: part[0], pieces)


def carried_in(x, axis, combine, identity):
    peers, here = (lax.axis_size(axis), lax.axis_index(axis))
    passed = jnp.arange(peers) < here

    def kept(part, zero, own):
        part = jnp.where(
            passed.reshape(-1, *(1 for _ in own.shape)), part, jnp.asarray(zero, own.dtype)
        )
        return part

    pieces = sent_to_all(x, axis)
    return joined_by_halves(kept(pieces, identity, x), combine)


def collected_together(x, axis):
    leaves = jax.tree.leaves(x)
    sequence = sorted(range(len(leaves)), key=lambda k: -leaves[k].size)
    width = (1, *leaves[sequence[0]].shape)[-1]
    lines = [
        jnp.pad(leaves[k].reshape(-1), (0, -leaves[k].size % width)).reshape(-1, width)
        for k in sequence
    ]
    both, at, found = (sent_to_all(jnp.concatenate(lines), axis), 0, {})
    for k, line in zip(sequence, lines):
        piece = both[:, at : at + len(line)].reshape(len(both), -1)
        found[k] = piece[:, : leaves[k].size].reshape(-1, *leaves[k].shape)
        at += len(line)
    numbers = iter(range(len(leaves)))
    return jax.tree.map(lambda _: found[next(numbers)], x)


def combined_all(x, axis, combine):
    pieces = collected_together(x, axis)
    return joined_by_halves(pieces, combine)


def add_counts(earlier, later):
    return earlier + later


def join_mass(first, second):
    peak = jnp.maximum(first[0], second[0])
    return (peak, first[1] * jnp.exp(first[0] - peak) + second[1] * jnp.exp(second[0] - peak))


def select_rows(index, table_rows, table_vols):
    columns = jnp.arange(table_rows.shape[1], dtype=jnp.int32)
    picker = (index[:, :, None] == columns[None, None, :]).astype(jnp.bfloat16)
    rows_out = jnp.einsum(
        "psr,prk->psk", picker, table_rows, preferred_element_type=jnp.float32
    ).astype(jnp.bfloat16)
    vols_out = jnp.einsum(
        "psr,pr->ps", picker, table_vols, preferred_element_type=jnp.float32
    ).astype(jnp.bfloat16)
    return (rows_out, vols_out)


def local(
    states,
    log_vol,
    transition,
    loading,
    yields,
    state_noise,
    vol_noise,
    vol_mean,
    vol_persist,
    vol_scale,
    obs_prec,
    prior_loglik,
    ancestors,
    counts,
    local_anc,
):
    p_dev, s_dev, width = states.shape
    group = lax.axis_index("theta")
    shard = lax.axis_index("state")
    mine = lax.dynamic_slice_in_dim(ancestors, group * p_dev, p_dev)
    offset_group = mine // p_dev - group
    local_source = mine % p_dev
    joined = jnp.concatenate([transition, states], axis=1)
    arrived, vols_arrived = (
        padded(joined, (("theta", 0),), p_dev),
        padded(log_vol, (("theta", 0),), p_dev),
    )
    picked = (offset_group + 1) * p_dev + local_source
    moved = jnp.take(arrived, picked, axis=0)
    vols = jnp.take(vols_arrived, picked, axis=0)
    matrix = moved[:, :width]
    cloud = moved[:, width:]
    center = jnp.take(vol_mean, mine)[:, None]
    persist = jnp.take(vol_persist, mine)[:, None]
    spread = jnp.take(vol_scale, mine)[:, None]
    precision = jnp.take(obs_prec, mine)
    total = jnp.take(prior_loglik, mine)
    number = counts[:, :, 0]
    starts = carried_in(number, "state", add_counts, jnp.zeros_like(number))
    margin = s_dev // 4
    shard_slots = local_anc.shape[2]
    global_rows = shard * s_dev + jnp.arange(s_dev, dtype=jnp.int32)
    whole_rows = s_dev * lax.axis_size("state")
    peaks = []
    masses = []
    for step in range(STEPS):
        chosen = local_anc[step]
        count = number[step]
        first = starts[step]
        tail_slots = count[:, None] - margin + jnp.arange(margin, dtype=jnp.int32)[None, :]
        sending = jnp.concatenate(
            [chosen[:, :margin], jnp.take_along_axis(chosen, tail_slots, axis=1)], axis=1
        )
        edge_states, edge_vols = select_rows(sending, cloud, vols)
        got_states, got_vols = (
            padded(edge_states, (("state", 1),), margin),
            padded(edge_vols, (("state", 1),), margin),
        )
        table_states = jnp.concatenate(
            [got_states[:, :margin], cloud, got_states[:, 3 * margin :]], axis=1
        )
        table_vols = jnp.concatenate(
            [got_vols[:, :margin], vols, got_vols[:, 3 * margin :]], axis=1
        )
        relative = global_rows[None, :] - first[:, None]
        own_rows = jnp.take_along_axis(chosen, jnp.clip(relative, 0, shard_slots - 1), axis=1)
        source = jnp.where(
            relative < 0,
            relative + margin,
            jnp.where(
                relative < count[:, None],
                margin + own_rows,
                margin + s_dev + relative - count[:, None],
            ),
        )
        cloud, vols_picked = select_rows(source, table_states, table_vols)
        vols_now = vols_picked.astype(jnp.float32)
        vols_now = center + persist * (vols_now - center) + spread * vol_noise[step][None, :]
        drift = jnp.einsum("psk,pkl->psl", cloud, matrix, preferred_element_type=jnp.float32)
        cloud = (
            drift
            + jnp.exp(0.5 * vols_now)[:, :, None] * state_noise[step][None].astype(jnp.float32)
        ).astype(jnp.bfloat16)
        vols = vols_now.astype(jnp.bfloat16)
        predicted = jnp.einsum("psk,km->psm", cloud, loading, preferred_element_type=jnp.float32)
        misfit = yields[step][None, None, :] - predicted
        weights_log = (
            -0.5 * precision[:, None] * jnp.sum(misfit * misfit, axis=2)
            + 0.5 * M * jnp.log(precision)[:, None]
        )
        local_peak = jnp.max(weights_log, axis=1)
        peaks.append(local_peak)
        masses.append(jnp.sum(jnp.exp(weights_log - local_peak[:, None]), axis=1))
    peak, mass = combined_all((jnp.stack(peaks), jnp.stack(masses)), "state", join_mass)
    total = total + jnp.sum(peak + jnp.log(mass) - math.log(whole_rows), axis=0)
    return (cloud, vols, total)


def solution(mesh):
    placed = (
        P("theta", "state", None),
        P("theta", "state"),
        P("theta", None, None),
        P(),
        P(),
        P(None, "state", None),
        P(None, "state"),
        P(),
        P(),
        P(),
        P(),
        P(),
        P(),
        P(None, "theta", "state"),
        P(None, "theta", "state"),
    )
    return jax.shard_map(
        local,
        mesh=mesh,
        in_specs=placed,
        out_specs=(P("theta", "state", None), P("theta", "state"), P("theta")),
        check_vma=False,
    )
```

profile of v0, /device:TPU:1, one launch (start us, length us, event | category | flops | bytes accessed | tf_op | source)
XLA Modules:
  0.0 280.5 jit_solution(6434757883985189157)
XLA Ops:
  0.7 4.1 %collective-permute-start.4 = (bf16[8,512]{1,0:T(8,128)(2,1)}, bf16[8,512]{1,0:T(8,128)(2,1)S(1)}, u32[]{:S(2)}, u32[]{:S(2)}) collective-permute-start(bf16[8,512]{1,0:T(8,128)(2,1)} %param.22), channel_id=1, source_target_pairs={{0,64},{64,128},{128,192},{1,65},{65,129},{129,193},{2,66},{66,130... | collective-permute-start | bytes 24584 | tf_op jit(solution)/shard_map/ppermute | solution.py:17
  4.8 1.3 collective-permute-start.5
  6.1 1.3 constant_dynamic-update-slice_fusion.1
  7.6 5.6 %collective-permute-start = (bf16[8,768,256]{2,1,0:T(8,128)(2,1)S(1)}, bf16[8,768,256]{2,1,0:T(8,128)(2,1)}, u32[]{:S(2)}, u32[]{:S(2)}) collective-permute-start(bf16[8,768,256]{2,1,0:T(8,128)(2,1)S(1)} %constant_dynamic-update-slice_fusion), channel_id=1, source_target_pairs={{0,64},{64,128},{128,192},{1,65},{65,129},{129,193},{2,66},{66,130... | collective-permute-start | bytes 9437192 | tf_op jit(solution)/shard_map/ppermute | solution.py:17
  13.2 1.3 collective-permute-start.1
  14.5 0.7 broadcast_in_dim.48
  15.2 13.3 %all-to-all-start = ((s32[64,3,8]{2,1,0:T(4,128)}), s32[64,3,8]{2,1,0:T(4,128)S(1)}, u32[]{:S(2)}, u32[]{:S(2)}) async-start(s32[64,3,8]{2,1,0:T(4,128)} %broadcast_in_dim.48), calls=%async_computation | async-start | bytes 262144 | tf_op jit(solution)/shard_map/all_to_all | solution.py:27
  28.5 0.6 slice_bitcast_fusion.6
  29.4 6.7 %gather_fusion.7 = s32[1024]{0:T(1024)S(1)} fusion(s32[8,768]{1,0:T(8,128)S(1)} %get-tuple-element.34, s32[1024]{0:T(1024)S(1)} %get-tuple-element.75), kind=kCustom, calls=%fused_computation.6.clone | custom fusion | bytes 16384 | tf_op jit(solution)/shard_map/jit(take_along_axis)/gather | solution.py:147
  36.2 1.2 gather_fusion.8
  37.4 1.2 gather_fusion.9
  38.6 1.2 gather_fusion.10
  39.7 1.2 gather_fusion.12
  40.9 2.3 bitcast_convert_fusion.2
  43.2 6.7 %gather_fusion.5 = s32[1024]{0:T(1024)S(1)} fusion(s32[8,768]{1,0:T(8,128)S(1)} %get-tuple-element.36, s32[1024]{0:T(1024)S(1)} %get-tuple-element.76), kind=kCustom, calls=%fused_computation.5.clone | custom fusion | bytes 16384 | tf_op jit(solution)/shard_map/jit(take_along_axis)/gather | solution.py:147
  50.1 6.7 %gather_fusion.3 = s32[1024]{0:T(1024)S(1)} fusion(s32[8,768]{1,0:T(8,128)S(1)} %get-tuple-element.35, s32[1024]{0:T(1024)S(1)} %fusion.110), kind=kCustom, calls=%fused_computation.1.clone | custom fusion | bytes 16384 | tf_op jit(solution)/shard_map/jit(take_along_axis)/gather | solution.py:147
  56.9 0.7 broadcast_multiply_fusion
  58.4 1.1 fusion.12
  59.5 3.5 %collective-permute-start.6 = (bf16[8,128]{1,0:T(8,128)(2,1)S(1)}, bf16[8,128]{1,0:T(8,128)(2,1)S(1)}, u32[]{:S(2)}, u32[]{:S(2)}) collective-permute-start(bf16[8,128]{1,0:T(8,128)(2,1)S(1)} %get-tuple-element.50), channel_id=1, source_target_pairs={{0,1},{1,2},{2,3},{3,4},{4,5},{5,6},{6,7},{7,8},{8,9},{9,10},{10,1... | collective-permute-start | bytes 6152 | tf_op jit(solution)/shard_map/ppermute | solution.py:17
  63.1 1.9 collective-permute-start.7
  65.1 3.3 %collective-permute-done.7 = bf16[8,128]{1,0:T(8,128)(2,1)S(1)} collective-permute-done((bf16[8,128]{1,0:T(8,128)(2,1)S(1)}, bf16[8,128]{1,0:T(8,128)(2,1)S(1)}, u32[]{:S(2)}, u32[]{:S(2)}) %collective-permute-start.7) | collective-permute-done | bytes 2080 | tf_op jit(solution)/shard_map/ppermute | solution.py:20
  68.7 25.3 %gather_fusion.2 = s32[4096]{0:T(1024)S(1)} fusion(s32[8,768]{1,0:T(8,128)S(1)} %get-tuple-element.35, s32[4096]{0:T(1024)S(1)} %bitcast.156), kind=kCustom, calls=%fused_computation.clone | custom fusion | bytes 65536 | tf_op jit(solution)/shard_map/jit(take_along_axis)/gather | solution.py:161
  94.1 25.3 %gather_fusion.4 = s32[4096]{0:T(1024)S(1)} fusion(s32[8,768]{1,0:T(8,128)S(1)} %get-tuple-element.36, s32[4096]{0:T(1024)S(1)} %bitcast.157), kind=kCustom, calls=%fused_computation.3.clone | custom fusion | bytes 65536 | tf_op jit(solution)/shard_map/jit(take_along_axis)/gather | solution.py:161
  119.4 25.3 %gather_fusion.6 = s32[4096]{0:T(1024)S(1)} fusion(s32[8,768]{1,0:T(8,128)S(1)} %get-tuple-element.34, s32[4096]{0:T(1024)S(1)} %bitcast.158), kind=kCustom, calls=%fused_computation.4.clone | custom fusion | bytes 65536 | tf_op jit(solution)/shard_map/jit(take_along_axis)/gather | solution.py:161
  144.9 2.8 %fusion = bf16[8,1,512]{2,1,0:T(2,128)(2,1)S(1)} fusion(s32[8,512]{1,0:T(8,128)S(1)} %get-tuple-element.55, bf16[8,768,1]{1,0,2:T(8,128)(2,1)S(1)} %maximum_bitcast_fusion), kind=kOutput, calls=%fused_computation.14 | convolution fusion | flops 9437184 | bytes 36864 | tf_op jit(solution)/shard_map/psr,pr->ps/dot_general | solution.py:89
  147.8 1.1 fusion.14
  148.9 1.9 collective-permute-start.10
  150.9 2.4 collective-permute-start.11
  153.3 2.5 collective-permute-done.11
  155.8 2.8 %fusion.2 = bf16[8,1,512]{2,1,0:T(2,128)(2,1)S(1)} fusion(s32[8,512]{1,0:T(8,128)S(1)} %get-tuple-element.57, bf16[8,768,1]{1,0,2:T(8,128)(2,1)S(1)} %maximum_bitcast_fusion.1), kind=kOutput, calls=%fused_computation.17 | convolution fusion | flops 9437184 | bytes 36864 | tf_op jit(solution)/shard_map/psr,pr->ps/dot_general | solution.py:89
  158.6 7.7 %pad_maximum_fusion = bf16[24,768,256]{2,1,0:T(8,128)(2,1)} fusion(bf16[8,768,256]{2,1,0:T(8,128)(2,1)} %collective-permute-done.1, bf16[8,768,256]{2,1,0:T(8,128)(2,1)S(1)} %constant_dynamic-update-slice_fusion, bf16[8,768,256]{2,1,0:T(8,128)(2,1)} %collective-permute-done), kind=kLoop, calls=%fused_computation.22 | loop fusion | flops 9437184 | bytes 18874368 | tf_op jit(solution)/shard_map/concatenate | solution.py:21
  166.3 4.4 %gather_fusion = bf16[8,768,256]{2,1,0:T(8,128)(2,1)S(1)} fusion(bf16[24,768,256]{2,1,0:T(8,128)(2,1)} %pad_maximum_fusion, s32[1024]{0:T(1024)S(1)} %pad_clamp_fusion.1), kind=kCustom, calls=%fused_computation.11 | custom fusion | bytes 6291488 | tf_op jit(solution)/shard_map/jit(_take)/gather | solution.py:124
  171.1 1.1 fusion.44
  172.4 2.1 collective-permute-start.2
  174.4 2.4 collective-permute-start.3
  176.9 1.1 fusion.16
  178.1 3.2 %collective-permute-start.14 = (bf16[8,128]{1,0:T(8,128)(2,1)S(1)}, bf16[8,128]{1,0:T(8,128)(2,1)S(1)}, u32[]{:S(2)}, u32[]{:S(2)}) collective-permute-start(bf16[8,128]{1,0:T(8,128)(2,1)S(1)} %get-tuple-element.46), channel_id=1, source_target_pairs={{0,1},{1,2},{2,3},{3,4},{4,5},{5,6},{6,7},{7,8},{8,9},{9,10},{10,1... | collective-permute-start | bytes 6152 | tf_op jit(solution)/shard_map/ppermute | solution.py:17
  181.2 2.1 collective-permute-start.15
  183.5 1.4 collective-permute-done.3
  184.9 0.8 copy-done.27
  185.7 5.0 %add_convert_fusion.2 = bf16[8,512,256]{2,1,0:T(8,128)(2,1)} fusion(f32[512,256]{1,0:T(8,128)S(1)} %copy-done.9, f32[8,512]{1,0:T(8,128)S(1)} %get-tuple-element.39, s32[8,512]{1,0:T(8,128)S(1)} %get-tuple-element.55, bf16[8,128,256]{2,1,0:T(8,128)(2,1)} %copy-done.27, bf16[8,512,256]{2,1,0:T(8,128)(2,1)S(1)} %slice.335, ...), kind=kOutput, calls=%fused_computation.31 | convolution fusion | flops 2164260864 | bytes 6848512 | tf_op jit(solution)/shard_map/psk,pkl->psl/dot_general | solution.py:174
  190.8 2.6 fusion.43
  193.5 2.5 collective-permute-start.8
  196.0 2.1 collective-permute-start.9
  198.2 2.8 %fusion.4 = bf16[8,1,512]{2,1,0:T(2,128)(2,1)S(1)} fusion(s32[8,512]{1,0:T(8,128)S(1)} %get-tuple-element.56, bf16[8,768,1]{1,0,2:T(8,128)(2,1)S(1)} %maximum_bitcast_fusion.2), kind=kOutput, calls=%fused_computation.20 | convolution fusion | flops 9437184 | bytes 36864 | tf_op jit(solution)/shard_map/psr,pr->ps/dot_general | solution.py:89
  201.1 1.1 collective-permute-done.8
  202.1 5.0 %collective-permute-done.9 = bf16[8,128,256]{2,1,0:T(8,128)(2,1)S(1)} collective-permute-done((bf16[8,128,256]{2,1,0:T(8,128)(2,1)S(1)}, bf16[8,128,256]{2,1,0:T(8,128)(2,1)S(1)}, u32[]{:S(2)}, u32[]{:S(2)}) %collective-permute-start.9) | collective-permute-done | bytes 524320 | tf_op jit(solution)/shard_map/ppermute | solution.py:20
  207.1 0.8 copy-done.28
  207.9 5.5 %add_convert_fusion.1 = bf16[8,512,256]{2,1,0:T(8,128)(2,1)} fusion(f32[512,256]{1,0:T(8,128)} %get-tuple-element.31, f32[8,512]{1,0:T(8,128)S(1)} %get-tuple-element.41, s32[8,512]{1,0:T(8,128)S(1)} %get-tuple-element.57, bf16[8,128,256]{2,1,0:T(8,128)(2,1)} %copy-done.28, bf16[8,512,256]{2,1,0:T(8,128)(2,1)} %add_convert_fusion.2, ...), kind=kOutput, calls=%fused_computation.30 | convolution fusion | flops 2164260864 | bytes 6848512 | tf_op jit(solution)/shard_map/psk,pkl->psl/dot_general | solution.py:174
  213.4 2.8 fusion.42
  216.2 2.1 collective-permute-start.12
  218.3 2.4 collective-permute-start.13
  220.7 0.7 fusion.104
  221.4 0.8 multiply_reduce_fusion.2
  222.3 0.8 multiply_reduce_fusion.1
  223.1 1.3 collective-permute-done.12
  224.4 6.5 %collective-permute-done.13 = bf16[8,128,256]{2,1,0:T(8,128)(2,1)S(1)} collective-permute-done((bf16[8,128,256]{2,1,0:T(8,128)(2,1)S(1)}, bf16[8,128,256]{2,1,0:T(8,128)(2,1)S(1)}, u32[]{:S(2)}, u32[]{:S(2)}) %collective-permute-start.13) | collective-permute-done | bytes 524320 | tf_op jit(solution)/shard_map/ppermute | solution.py:20
  231.0 0.8 copy-done.30
  231.8 5.4 %add_convert_fusion = bf16[8,512,256]{2,1,0:T(8,128)(2,1)} fusion(f32[512,256]{1,0:T(8,128)} %get-tuple-element.30, f32[8,512]{1,0:T(8,128)S(1)} %get-tuple-element.38, s32[8,512]{1,0:T(8,128)S(1)} %get-tuple-element.56, bf16[8,128,256]{2,1,0:T(8,128)(2,1)} %copy-done.30, bf16[8,512,256]{2,1,0:T(8,128)(2,1)} %add_convert_fusion.1, ...), kind=kOutput, calls=%fused_computation.29 | convolution fusion | flops 2164260864 | bytes 6848512 | tf_op jit(solution)/shard_map/psk,pkl->psl/dot_general | solution.py:174
  237.2 2.4 multiply_reduce_fusion
  240.3 0.7 broadcast_in_dim.55
  241.1 25.5 %all-to-all-start.1 = ((f32[64,6,8]{2,1,0:T(8,128)}), f32[64,6,8]{2,1,0:T(8,128)S(1)}, u32[]{:S(2)}, u32[]{:S(2)}) async-start(f32[64,6,8]{2,1,0:T(8,128)} %broadcast_in_dim.55), calls=%async_computation.1 | async-start | bytes 524288 | tf_op jit(solution)/shard_map/all_to_all | solution.py:27
  266.5 0.6 gather_fusion.11
  267.2 12.4 %all-to-all-done.1 = f32[64,6,8]{2,1,0:T(8,128)S(1)} async-done(((f32[64,6,8]{2,1,0:T(8,128)}), f32[64,6,8]{2,1,0:T(8,128)S(1)}, u32[]{:S(2)}, u32[]{:S(2)}) %all-to-all-start.1) | async-done | bytes 12320 | tf_op jit(solution)/shard_map/all_to_all | solution.py:27
  (144 shorter events, 4.5 us)
Async XLA Ops:
  0.6 220.8 %copy-start = (bf16[256,128]{1,0:T(8,128)(2,1)S(1)}, bf16[256,128]{1,0:T(8,128)(2,1)}, u32[]{:S(2)}) copy-start(bf16[256,128]{1,0:T(8,128)(2,1)} %param.24) | copy-start | bytes 196612
  0.6 6.7 %copy-start.8 = (bf16[8,512,256]{2,1,0:T(8,128)(2,1)S(1)}, bf16[8,512,256]{2,1,0:T(8,128)(2,1)}, u32[]{:S(2)}) copy-start(bf16[8,512,256]{2,1,0:T(8,128)(2,1)} %param.21) | copy-start | bytes 6291460
  0.7 13.8 %copy-start.11 = (s32[3,8,1]{1,2,0:T(1,128)S(1)}, s32[3,8,1]{1,2,0:T(1,128)}, u32[]{:S(2)}) copy-start(s32[3,8,1]{1,2,0:T(1,128)} %param.34) | copy-start | bytes 292
  0.7 28.4 %copy-start.16 = (s32[32]{0:T(128)S(1)}, s32[32]{0:T(128)}, u32[]{:S(2)}) copy-start(s32[32]{0:T(128)} %param.33) | copy-start | bytes 388
  0.7 28.6 %copy-start.10 = (s32[3,8,768]{2,1,0:T(8,128)S(1)}, s32[3,8,768]{2,1,0:T(8,128)}, u32[]{:S(2)}) copy-start(s32[3,8,768]{2,1,0:T(8,128)} %param.35) | copy-start | bytes 221188
  0.7 57.0 %collective-permute-start.4 = (bf16[8,512]{1,0:T(8,128)(2,1)}, bf16[8,512]{1,0:T(8,128)(2,1)S(1)}, u32[]{:S(2)}, u32[]{:S(2)}) collective-permute-start(bf16[8,512]{1,0:T(8,128)(2,1)} %param.22), channel_id=1, source_target_pairs={{0,64},{64,128},{128,192},{1,65},{65,129},{129,193},{2,66},{66,130... | collective-permute-start | bytes 24584 | tf_op jit(solution)/shard_map/ppermute | solution.py:17
  4.8 53.0 %collective-permute-start.5 = (bf16[8,512]{1,0:T(8,128)(2,1)}, bf16[8,512]{1,0:T(8,128)(2,1)S(1)}, u32[]{:S(2)}, u32[]{:S(2)}) collective-permute-start(bf16[8,512]{1,0:T(8,128)(2,1)} %param.22), channel_id=1, source_target_pairs={{64,0},{128,64},{192,128},{65,1},{129,65},{193,129},{66,2},{130,66... | collective-permute-start | bytes 24584 | tf_op jit(solution)/shard_map/ppermute | solution.py:20
  7.5 28.7 %copy-start.1 = (f32[32]{0:T(128)S(1)}, f32[32]{0:T(128)}, u32[]{:S(2)}) copy-start(f32[32]{0:T(128)} %param.28) | copy-start | bytes 388
  7.5 29.9 %copy-start.2 = (f32[32]{0:T(128)S(1)}, f32[32]{0:T(128)}, u32[]{:S(2)}) copy-start(f32[32]{0:T(128)} %param.29) | copy-start | bytes 388
  7.6 151.1 %collective-permute-start = (bf16[8,768,256]{2,1,0:T(8,128)(2,1)S(1)}, bf16[8,768,256]{2,1,0:T(8,128)(2,1)}, u32[]{:S(2)}, u32[]{:S(2)}) collective-permute-start(bf16[8,768,256]{2,1,0:T(8,128)(2,1)S(1)} %constant_dynamic-update-slice_fusion), channel_id=1, source_target_pairs={{0,64},{64,128},{128,192},{1,65},{65,129},{129,193},{2,66},{66,130... | collective-permute-start | bytes 9437192 | tf_op jit(solution)/shard_map/ppermute | solution.py:17
  13.2 145.4 %collective-permute-start.1 = (bf16[8,768,256]{2,1,0:T(8,128)(2,1)S(1)}, bf16[8,768,256]{2,1,0:T(8,128)(2,1)}, u32[]{:S(2)}, u32[]{:S(2)}) collective-permute-start(bf16[8,768,256]{2,1,0:T(8,128)(2,1)S(1)} %constant_dynamic-update-slice_fusion), channel_id=1, source_target_pairs={{64,0},{128,64},{192,128},{65,1},{129,65},{193,129},{66,2},{130,66... | collective-permute-start | bytes 9437192 | tf_op jit(solution)/shard_map/ppermute | solution.py:20
  15.2 23.4 %copy-start.3 = (f32[32]{0:T(128)S(1)}, f32[32]{0:T(128)}, u32[]{:S(2)}) copy-start(f32[32]{0:T(128)} %param.30) | copy-start | bytes 388
  15.2 53.2 %all-to-all-start = ((s32[64,3,8]{2,1,0:T(4,128)}), s32[64,3,8]{2,1,0:T(4,128)S(1)}, u32[]{:S(2)}, u32[]{:S(2)}) async-start(s32[64,3,8]{2,1,0:T(4,128)} %broadcast_in_dim.48), calls=%async_computation | async-start | bytes 262144 | tf_op jit(solution)/shard_map/all_to_all | solution.py:27
  28.5 0.9 copy-start.14
  29.4 10.3 %copy-start.4 = (f32[32]{0:T(128)S(1)}, f32[32]{0:T(128)}, u32[]{:S(2)}) copy-start(f32[32]{0:T(128)} %param.31) | copy-start | bytes 388
  29.4 11.5 %copy-start.13 = (f32[3,512]{1,0:T(4,128)S(1)}, f32[3,512]{1,0:T(4,128)}, u32[]{:S(2)}) copy-start(f32[3,512]{1,0:T(4,128)} %param.27) | copy-start | bytes 18436
  40.9 9.0 %copy-start.15 = (s32[8]{0:T(128)S(1)}, s32[8]{0:T(128)}, u32[]{:S(2)}) copy-start(s32[8]{0:T(128)} %copy-done.14) | copy-start | bytes 100
  49.9 7.0 %copy-start.17 = (s32[32]{0:T(128)S(1)}, s32[32]{0:T(128)}, u32[]{:S(2)}) copy-start(s32[32]{0:T(128)} %param.33) | copy-start | bytes 388
  49.9 7.0 %copy-start.22 = (f32[8]{0:T(128)S(1)}, f32[8]{0:T(128)}, u32[]{:S(2)}) copy-start(f32[8]{0:T(128)} %gather_fusion.8) | copy-start | bytes 100
  49.9 7.0 %copy-start.23 = (f32[8]{0:T(128)S(1)}, f32[8]{0:T(128)}, u32[]{:S(2)}) copy-start(f32[8]{0:T(128)} %gather_fusion.9) | copy-start | bytes 100
  49.9 7.8 %copy-start.12 = (bf16[8,512]{1,0:T(8,128)(2,1)S(1)}, bf16[8,512]{1,0:T(8,128)(2,1)}, u32[]{:S(2)}) copy-start(bf16[8,512]{1,0:T(8,128)(2,1)} %param.22) | copy-start | bytes 24580
  50.0 6.9 %copy-start.24 = (f32[8]{0:T(128)S(1)}, f32[8]{0:T(128)}, u32[]{:S(2)}) copy-start(f32[8]{0:T(128)} %gather_fusion.10) | copy-start | bytes 100
  59.5 5.6 %collective-permute-start.6 = (bf16[8,128]{1,0:T(8,128)(2,1)S(1)}, bf16[8,128]{1,0:T(8,128)(2,1)S(1)}, u32[]{:S(2)}, u32[]{:S(2)}) collective-permute-start(bf16[8,128]{1,0:T(8,128)(2,1)S(1)} %get-tuple-element.50), channel_id=1, source_target_pairs={{0,1},{1,2},{2,3},{3,4},{4,5},{5,6},{6,7},{7,8},{8,9},{9,10},{10,1... | collective-permute-start | bytes 6152 | tf_op jit(solution)/shard_map/ppermute | solution.py:17
  63.1 5.3 %collective-permute-start.7 = (bf16[8,128]{1,0:T(8,128)(2,1)S(1)}, bf16[8,128]{1,0:T(8,128)(2,1)S(1)}, u32[]{:S(2)}, u32[]{:S(2)}) collective-permute-start(bf16[8,128]{1,0:T(8,128)(2,1)S(1)} %get-tuple-element.51), channel_id=1, source_target_pairs={{1,0},{2,1},{3,2},{4,3},{5,4},{6,5},{7,6},{8,7},{9,8},{10,9},{11,1... | collective-permute-start | bytes 6152 | tf_op jit(solution)/shard_map/ppermute | solution.py:20
  119.4 25.3 %copy-start.19 = (s32[8]{0:T(128)S(1)}, s32[8]{0:T(128)}, u32[]{:S(2)}) copy-start(s32[8]{0:T(128)} %get-tuple-element.67) | copy-start | bytes 100
  119.4 25.3 %copy-start.20 = (s32[8]{0:T(128)S(1)}, s32[8]{0:T(128)}, u32[]{:S(2)}) copy-start(s32[8]{0:T(128)} %get-tuple-element.68) | copy-start | bytes 100
  119.4 25.3 %copy-start.21 = (s32[8]{0:T(128)S(1)}, s32[8]{0:T(128)}, u32[]{:S(2)}) copy-start(s32[8]{0:T(128)} %get-tuple-element.69) | copy-start | bytes 100
  148.9 4.4 %collective-permute-start.10 = (bf16[8,128]{1,0:T(8,128)(2,1)S(1)}, bf16[8,128]{1,0:T(8,128)(2,1)S(1)}, u32[]{:S(2)}, u32[]{:S(2)}) collective-permute-start(bf16[8,128]{1,0:T(8,128)(2,1)S(1)} %get-tuple-element.48), channel_id=1, source_target_pairs={{0,1},{1,2},{2,3},{3,4},{4,5},{5,6},{6,7},{7,8},{8,9},{9,10},{10,1... | collective-permute-start | bytes 6152 | tf_op jit(solution)/shard_map/ppermute | solution.py:17
  150.9 4.9 %collective-permute-start.11 = (bf16[8,128]{1,0:T(8,128)(2,1)S(1)}, bf16[8,128]{1,0:T(8,128)(2,1)S(1)}, u32[]{:S(2)}, u32[]{:S(2)}) collective-permute-start(bf16[8,128]{1,0:T(8,128)(2,1)S(1)} %get-tuple-element.49), channel_id=1, source_target_pairs={{1,0},{2,1},{3,2},{4,3},{5,4},{6,5},{7,6},{8,7},{9,8},{10,9},{11,1... | collective-permute-start | bytes 6152 | tf_op jit(solution)/shard_map/ppermute | solution.py:20
  171.1 12.2 %copy-start.6 = (bf16[8,768,256]{2,1,0:T(8,128)(2,1)}, bf16[8,768,256]{2,1,0:T(8,128)(2,1)S(1)}, u32[]{:S(2)}) copy-start(bf16[8,768,256]{2,1,0:T(8,128)(2,1)S(1)} %broadcast_select_fusion) | copy-start | bytes 9437188
  172.3 13.4 %copy-start.9 = (f32[512,256]{1,0:T(8,128)S(1)}, f32[512,256]{1,0:T(8,128)}, u32[]{:S(2)}) copy-start(f32[512,256]{1,0:T(8,128)} %get-tuple-element.29) | copy-start | bytes 1572868
  172.4 11.2 %collective-permute-start.2 = (bf16[8,128,256]{2,1,0:T(8,128)(2,1)S(1)}, bf16[8,128,256]{2,1,0:T(8,128)(2,1)S(1)}, u32[]{:S(2)}, u32[]{:S(2)}) collective-permute-start(bf16[8,128,256]{2,1,0:T(8,128)(2,1)S(1)} %get-tuple-element.27), channel_id=1, source_target_pairs={{0,1},{1,2},{2,3},{3,4},{4,5},{5,6},{6,7},{7,8},{8,9},{9,10},{10,1... | collective-permute-start | bytes 1572872 | tf_op jit(solution)/shard_map/ppermute | solution.py:17
  174.4 10.5 %collective-permute-start.3 = (bf16[8,128,256]{2,1,0:T(8,128)(2,1)S(1)}, bf16[8,128,256]{2,1,0:T(8,128)(2,1)S(1)}, u32[]{:S(2)}, u32[]{:S(2)}) collective-permute-start(bf16[8,128,256]{2,1,0:T(8,128)(2,1)S(1)} %get-tuple-element.28), channel_id=1, source_target_pairs={{1,0},{2,1},{3,2},{4,3},{5,4},{6,5},{7,6},{8,7},{9,8},{10,9},{11,1... | collective-permute-start | bytes 1572872 | tf_op jit(solution)/shard_map/ppermute | solution.py:20
  178.1 20.1 %collective-permute-start.14 = (bf16[8,128]{1,0:T(8,128)(2,1)S(1)}, bf16[8,128]{1,0:T(8,128)(2,1)S(1)}, u32[]{:S(2)}, u32[]{:S(2)}) collective-permute-start(bf16[8,128]{1,0:T(8,128)(2,1)S(1)} %get-tuple-element.46), channel_id=1, source_target_pairs={{0,1},{1,2},{2,3},{3,4},{4,5},{5,6},{6,7},{7,8},{8,9},{9,10},{10,1... | collective-permute-start | bytes 6152 | tf_op jit(solution)/shard_map/ppermute | solution.py:17
  181.2 17.0 %collective-permute-start.15 = (bf16[8,128]{1,0:T(8,128)(2,1)S(1)}, bf16[8,128]{1,0:T(8,128)(2,1)S(1)}, u32[]{:S(2)}, u32[]{:S(2)}) collective-permute-start(bf16[8,128]{1,0:T(8,128)(2,1)S(1)} %get-tuple-element.47), channel_id=1, source_target_pairs={{1,0},{2,1},{3,2},{4,3},{5,4},{6,5},{7,6},{8,7},{9,8},{10,9},{11,1... | collective-permute-start | bytes 6152 | tf_op jit(solution)/shard_map/ppermute | solution.py:20
  184.9 0.8 copy-start.27
  190.8 7.4 %copy-start.25 = (f32[3,128]{1,0:T(4,128)S(1)}, f32[3,128]{1,0:T(4,128)}, u32[]{:S(2)}) copy-start(f32[3,128]{1,0:T(4,128)} %param.25) | copy-start | bytes 4612
  193.5 14.4 %copy-start.7 = (bf16[8,768,256]{2,1,0:T(8,128)(2,1)S(1)}, bf16[8,768,256]{2,1,0:T(8,128)(2,1)}, u32[]{:S(2)}) copy-start(bf16[8,768,256]{2,1,0:T(8,128)(2,1)} %copy-done.6) | copy-start | bytes 9437188
  193.5 8.6 %collective-permute-start.8 = (bf16[8,128,256]{2,1,0:T(8,128)(2,1)S(1)}, bf16[8,128,256]{2,1,0:T(8,128)(2,1)S(1)}, u32[]{:S(2)}, u32[]{:S(2)}) collective-permute-start(bf16[8,128,256]{2,1,0:T(8,128)(2,1)S(1)} %get-tuple-element.25), channel_id=1, source_target_pairs={{0,1},{1,2},{2,3},{3,4},{4,5},{5,6},{6,7},{7,8},{8,9},{9,10},{10,1... | collective-permute-start | bytes 1572872 | tf_op jit(solution)/shard_map/ppermute | solution.py:17
  196.0 11.1 %collective-permute-start.9 = (bf16[8,128,256]{2,1,0:T(8,128)(2,1)S(1)}, bf16[8,128,256]{2,1,0:T(8,128)(2,1)S(1)}, u32[]{:S(2)}, u32[]{:S(2)}) collective-permute-start(bf16[8,128,256]{2,1,0:T(8,128)(2,1)S(1)} %get-tuple-element.26), channel_id=1, source_target_pairs={{1,0},{2,1},{3,2},{4,3},{5,4},{6,5},{7,6},{8,7},{9,8},{10,9},{11,1... | collective-permute-start | bytes 1572872 | tf_op jit(solution)/shard_map/ppermute | solution.py:20
  202.1 5.0 %copy-start.26 = (bf16[8,128,256]{2,1,0:T(8,128)(2,1)}, bf16[8,128,256]{2,1,0:T(8,128)(2,1)S(1)}, u32[]{:S(2)}) copy-start(bf16[8,128,256]{2,1,0:T(8,128)(2,1)S(1)} %collective-permute-done.8) | copy-start | bytes 1572868
  207.1 0.8 copy-start.28
  213.4 8.1 %copy-start.31 = (bf16[8,512,256]{2,1,0:T(8,128)(2,1)S(1)}, bf16[8,512,256]{2,1,0:T(8,128)(2,1)}, u32[]{:S(2)}) copy-start(bf16[8,512,256]{2,1,0:T(8,128)(2,1)} %add_convert_fusion.2) | copy-start | bytes 6291460
  216.2 6.1 %copy-start.32 = (bf16[8,512,256]{2,1,0:T(8,128)(2,1)S(1)}, bf16[8,512,256]{2,1,0:T(8,128)(2,1)}, u32[]{:S(2)}) copy-start(bf16[8,512,256]{2,1,0:T(8,128)(2,1)} %add_convert_fusion.1) | copy-start | bytes 6291460
  216.2 8.2 %collective-permute-start.12 = (bf16[8,128,256]{2,1,0:T(8,128)(2,1)S(1)}, bf16[8,128,256]{2,1,0:T(8,128)(2,1)S(1)}, u32[]{:S(2)}, u32[]{:S(2)}) collective-permute-start(bf16[8,128,256]{2,1,0:T(8,128)(2,1)S(1)} %get-tuple-element.23), channel_id=1, source_target_pairs={{0,1},{1,2},{2,3},{3,4},{4,5},{5,6},{6,7},{7,8},{8,9},{9,10},{10,1... | collective-permute-start | bytes 1572872 | tf_op jit(solution)/shard_map/ppermute | solution.py:17
  218.3 12.7 %collective-permute-start.13 = (bf16[8,128,256]{2,1,0:T(8,128)(2,1)S(1)}, bf16[8,128,256]{2,1,0:T(8,128)(2,1)S(1)}, u32[]{:S(2)}, u32[]{:S(2)}) collective-permute-start(bf16[8,128,256]{2,1,0:T(8,128)(2,1)S(1)} %get-tuple-element.24), channel_id=1, source_target_pairs={{1,0},{2,1},{3,2},{4,3},{5,4},{6,5},{7,6},{8,7},{9,8},{10,9},{11,1... | collective-permute-start | bytes 1572872 | tf_op jit(solution)/shard_map/ppermute | solution.py:20
  224.4 6.6 %copy-start.29 = (bf16[8,128,256]{2,1,0:T(8,128)(2,1)}, bf16[8,128,256]{2,1,0:T(8,128)(2,1)S(1)}, u32[]{:S(2)}) copy-start(bf16[8,128,256]{2,1,0:T(8,128)(2,1)S(1)} %collective-permute-done.12) | copy-start | bytes 1572868
  231.0 0.8 copy-start.30
  237.2 29.3 %copy-start.5 = (f32[32]{0:T(128)S(1)}, f32[32]{0:T(128)}, u32[]{:S(2)}) copy-start(f32[32]{0:T(128)} %param.32) | copy-start | bytes 388
  237.2 42.7 %copy-start.18 = (s32[32]{0:T(128)S(1)}, s32[32]{0:T(128)}, u32[]{:S(2)}) copy-start(s32[32]{0:T(128)} %param.33) | copy-start | bytes 388
  241.1 38.5 %all-to-all-start.1 = ((f32[64,6,8]{2,1,0:T(8,128)}), f32[64,6,8]{2,1,0:T(8,128)S(1)}, u32[]{:S(2)}, u32[]{:S(2)}) async-start(f32[64,6,8]{2,1,0:T(8,128)} %broadcast_in_dim.55), calls=%async_computation.1 | async-start | bytes 524288 | tf_op jit(solution)/shard_map/all_to_all | solution.py:27
where the time goes:
time: 282 us; the launch traced here: 280 us
  local copies, waits for them, and re-layouts  113 us (40%)
  starting transfers between devices  79.6 us (28%)
  matrix products  38.4 us (14%)
  waiting for transfers between devices  33.5 us (12%)
  other arithmetic  14.5 us (5%)
    gather x6, local copies, waits for them, and re-layouts, local(): jnp.take_along_axis(chosen, jnp.clip(relative, 0, shard_slots - 1), axis=1)  75.9 us
    all_to_all x2, starting transfers between devices, sent_to_all(): return lax.all_to_all(copies, axis, split_axis=0, concat_axis=0, tiled=True)  38.7 us
    ppermute x8, starting transfers between devices, padded(): lax.ppermute(lax.slice_in_dim(block, block.shape[dim] - width, None, axis...  24.9 us
    gather x3, local copies, waits for them, and re-layouts, local(): jnp.take_along_axis(chosen, tail_slots, axis=1)  20.1 us
    ppermute x8, waiting for transfers between devices, padded(): lax.ppermute(lax.slice_in_dim(block, 0, width, axis=dim), axis, backward)  18.7 us
    ppermute x8, starting transfers between devices, padded(): lax.ppermute(lax.slice_in_dim(block, 0, width, axis=dim), axis, backward)  16 us
    dot_general x3, matrix products, local(): jnp.einsum('psk,pkl->psl', cloud, matrix, preferred_element_type=jnp.floa...  16 us
    all_to_all x2, waiting for transfers between devices, sent_to_all(): return lax.all_to_all(copies, axis, split_axis=0, concat_axis=0, tiled=True)  12.4 us
  transfers between devices with their start and end apart: 18, of which 8 were waited for; matrix products, arithmetic and copies ran while one was open for 47% of the time, Pallas kernels for 0%

commit v1 on v0

v1 whole, which is shorter than its diff:
```python
import math

import jax
import jax.numpy as jnp
from jax import lax
from jax.experimental import pallas as pl
from jax.experimental.pallas import tpu as pltpu
from jax.sharding import PartitionSpec as P

K = 256
M = 128
PD = 8
SD = 512
STEPS = 3
MARGIN = 128
FRAME = SD + 2 * MARGIN
EXT = K + 16
KEEP = 4
TN = 4
JN = 64
WN = 8
F32 = jnp.float32
BF16 = jnp.bfloat16
I32 = jnp.int32
MESH = pl.DeviceIdType.MESH


def nt(a, b):
    return lax.dot_general(a, b, (((1,), (1,)), ((), ())), preferred_element_type=F32)


def nn(a, b):
    return lax.dot_general(a, b, (((1,), (0,)), ((), ())), preferred_element_type=F32)


def iota(shape, dim):
    return lax.broadcasted_iota(I32, shape, dim)


def eye(n):
    return jnp.where(iota((n, n), 0) == iota((n, n), 1), 1.0, 0.0).astype(BF16)


def kernel(
    anc, cnt, vm_s, vp_s, vs_s, op_s, pr_s,
    lv, ld, yl, vn, la, states, trans, noise,
    o_states, o_vol, o_ll,
    st, tr, nz, sc, sm, sv, rc, rm, rv,
    cT, own, mT, nT, lT, yb, eL, eR, hL, hR,
    ctile, c2tile, g1, g2, dref, eref, cz, stats, s1, s2, lvf, vf, osb, tmp, eyer,
    perm_s, src_s, rem_s, anc_s, pos_s, snd_s,
    ld_sem, th_ss, th_rs, tv_ss, tv_rs, hl_ss, hl_rs, g_ss, g_rs, out_sem,
):
    g = lax.axis_index("theta")
    j = lax.axis_index("state")
    z, w = j // WN, j % WN
    left, right = (j + JN - 1) % JN, (j + 1) % JN

    def dev(theta, state):
        return {"theta": theta, "state": state}

    barrier = pltpu.get_barrier_semaphore()

    def greet(theta, state):
        pl.semaphore_signal(
            barrier, inc=1, device_id=dev(theta, state), device_id_type=MESH
        )

    for o in range(1, 8):
        greet(g, ((z + o) % 8) * WN + w)
    for o in range(1, WN):
        greet(g, z * WN + (w + o) % WN)
    greet(g, left)
    greet(g, right)

    @pl.when(g > 0)
    def _():
        greet(g - 1, j)

    @pl.when(g < TN - 1)
    def _():
        greet(g + 1, j)

    load_st = pltpu.make_async_copy(states, st, ld_sem.at[0])
    load_tr = pltpu.make_async_copy(trans, tr, ld_sem.at[1])
    load_nz = pltpu.make_async_copy(noise, nz, ld_sem.at[2])
    load_st.start()
    load_tr.start()
    load_nz.start()

    a8 = [anc[g * PD + i] for i in range(PD)]
    off = [lax.shift_right_arithmetic(a, 3) - g for a in a8]
    below = [jnp.where(o == -1, 1, 0) for o in off]
    above = [jnp.where(o == 1, 1, 0) for o in off]
    nb, na, nl = 0, 0, 0
    rank_b, rank_a, rank_l = [], [], []
    for i in range(PD):
        rank_b.append(nb)
        rank_a.append(na)
        rank_l.append(nl)
        nb = nb + below[i]
        na = na + above[i]
        nl = nl + 1 - below[i] - above[i]
    free_b = KEEP - nb
    pos = []
    for i in range(PD):
        l = rank_l[i]
        home = jnp.where(l < free_b, 2 * (nb + l), 2 * (na + l - free_b) + 1)
        slot = jnp.where(
            below[i] == 1,
            2 * rank_b[i],
            jnp.where(above[i] == 1, 2 * rank_a[i] + 1, home),
        )
        pos.append(jnp.clip(slot, 0, PD - 1))
        pos_s[i] = pos[i]
    for n in range(PD):
        who, a = 0, 0
        for i in range(PD):
            hit = pos[i] == n
            who = jnp.where(hit, i, who)
            a = jnp.where(hit, a8[i], a)
        perm_s[n] = who
        anc_s[n] = a
        src_s[n] = a & (PD - 1)
        rem_s[n] = jnp.where(lax.shift_right_arithmetic(a, 3) == g, 0, 1)
    for d, peer in ((0, jnp.minimum(g + 1, TN - 1)), (1, jnp.maximum(g - 1, 0))):
        rank = 0
        chosen = [0] * KEEP
        for i in range(PD):
            a = anc[peer * PD + i]
            hit = jnp.where(lax.shift_right_arithmetic(a, 3) == g, 1, 0)
            for k in range(KEEP):
                take = jnp.where(rank == k, hit, 0)
                chosen[k] = jnp.where(take == 1, a & (PD - 1), chosen[k])
            rank = rank + hit
        for k in range(KEEP):
            snd_s[2 * k + d] = chosen[k]

    row8, lane8 = iota((PD, 128), 0), iota((PD, 128), 1)
    tile = jnp.zeros((PD, 128), I32)
    for t in range(STEPS):
        for p in range(PD):
            tile = jnp.where((row8 == p) & (lane8 == t), cnt[t * PD + p], tile)
    ctile[...] = tile
    lvf[...] = lv[...].astype(F32)
    for d in range(2):
        for k in range(KEEP):
            row = lvf[pl.ds(snd_s[2 * k + d], 1), :]
            sv[d, k : k + 1, :] = row
            sv[d, KEEP + k : KEEP + k + 1, :] = row
    load_st.wait()
    load_tr.wait()

    def fill(n, _):
        s = snd_s[n]
        sc[n] = st[s]
        sm[n] = tr[s]
        return 0

    def send_copy(n):
        peer = jnp.where(n % 2 == 0, g + 1, g - 1)
        c = pltpu.make_async_remote_copy(
            sc.at[n], rc.at[n], th_ss.at[0, n], th_rs.at[0, n],
            device_id=dev(peer, j), device_id_type=MESH,
        )
        m = pltpu.make_async_remote_copy(
            sm.at[n], rm.at[n], th_ss.at[1, n], th_rs.at[1, n],
            device_id=dev(peer, j), device_id_type=MESH,
        )
        return c, m

    def send_vol(d):
        peer = jnp.where(d == 0, g + 1, g - 1)
        return pltpu.make_async_remote_copy(
            sv.at[d], rv.at[d], tv_ss.at[d], tv_rs.at[d],
            device_id=dev(peer, j), device_id_type=MESH,
        )

    def group1(o, src, dst, u):
        return pltpu.make_async_remote_copy(
            src, dst.at[o], g_ss.at[u, o], g_rs.at[u, o],
            device_id=dev(g, z * WN + (w + o) % WN), device_id_type=MESH,
        )

    def group2(o, src, dst, u):
        return pltpu.make_async_remote_copy(
            src, dst.at[o], g_ss.at[u, o], g_rs.at[u, o],
            device_id=dev(g, ((z + o) % 8) * WN + w), device_id_type=MESH,
        )

    lax.fori_loop(0, 2, fill, 0)
    pl.semaphore_wait(
        barrier, 16 + jnp.where(g > 0, 1, 0) + jnp.where(g < TN - 1, 1, 0)
    )
    for o in range(1, WN):
        group1(o, ctile, g1, 0).start()

    def each_dir(fn):
        @pl.when(g < TN - 1)
        def _():
            fn(0)

        @pl.when(g > 0)
        def _():
            fn(1)

    def has_in(n):
        return jnp.where(n % 2 == 0, g > 0, g < TN - 1)

    def has_out(n):
        return jnp.where(n % 2 == 0, g < TN - 1, g > 0)

    each_dir(lambda d: send_vol(d).start())

    def start_pair(n, _):
        @pl.when(has_out(n))
        def _():
            c, m = send_copy(n)
            c.start()
            m.start()

        return 0

    lax.fori_loop(0, 2, start_pair, 0)
    lax.fori_loop(2, 2 * KEEP, fill, 0)
    lax.fori_loop(2, 2 * KEEP, start_pair, 0)

    eyer[...] = eye(K)
    load_nz.wait()
    for t in range(STEPS):
        nT[t] = nt(eyer[...], nz[t]).astype(BF16)
        yb[t] = jnp.transpose(jnp.broadcast_to(yl[t : t + 1, :], (M, M)))
    lT[...] = nt(eye(M), ld[...]).astype(BF16)
    stats[...] = jnp.zeros_like(stats)

    before = jnp.zeros((PD, 128), I32)
    whole = ctile[...]
    for o in range(1, WN):
        group1(o, ctile, g1, 0).wait_recv()
        got = g1[o]
        source = (w + WN - o) % WN
        before = before + jnp.where(source < w, got, 0)
        whole = whole + got
    c2tile[...] = whole
    for o in range(1, 8):
        group2(o, c2tile, g2, 1).start()
    for o in range(1, 8):
        group2(o, c2tile, g2, 1).wait_recv()
        source = (z + 8 - o) % 8
        before = before + jnp.where(source < z, g2[o], 0)
    first = before - SD * j
    for t in range(STEPS):
        d = jnp.broadcast_to(first[:, t : t + 1], (PD, 128))
        e = d + jnp.broadcast_to(tile[:, t : t + 1], (PD, 128))
        dref[t * PD : (t + 1) * PD, :] = d
        eref[t * PD : (t + 1) * PD, :] = e
        shift = jnp.concatenate([d + MARGIN] * (FRAME // 128), axis=1)
        x = la[t * PD : (t + 1) * PD, :]
        for b in range(9):
            x = jnp.where((shift & (1 << b)) != 0, pltpu.roll(x, 1 << b, 1), x)
        cz[t * PD : (t + 1) * PD, :] = x

    def halo(n, t):
        to_left = pltpu.make_async_remote_copy(
            eL.at[n, t], hR.at[n, t], hl_ss.at[0, n, t], hl_rs.at[0, n, t],
            device_id=dev(g, left), device_id_type=MESH,
        )
        to_right = pltpu.make_async_remote_copy(
            eR.at[n, t], hL.at[n, t], hl_ss.at[1, n, t], hl_rs.at[1, n, t],
            device_id=dev(g, right), device_id_type=MESH,
        )
        return to_left, to_right

    def build(n):
        @pl.when(has_in(n))
        def _():
            c, m = send_copy(n)
            c.wait_recv()
            m.wait_recv()

        src = src_s[n]
        remote = rem_s[n] == 1
        eyes = eyer[...]
        cloud = jnp.where(remote, rc[n].astype(F32), st[src].astype(F32)).astype(BF16)
        cT[n, 0:K, :] = nt(eyes, cloud).astype(BF16)
        mat = jnp.where(remote, rm[n].astype(F32), tr[src].astype(F32)).astype(BF16)
        mT[n] = nt(eyes, mat).astype(BF16)
        got = rv[n % 2, pl.ds(n // 2, 1), :]
        vol = jnp.where(remote, got, lvf[pl.ds(src, 1), :])
        cT[n, K:EXT, :] = jnp.broadcast_to(vol, (EXT - K, SD)).astype(BF16)

    def draw(n, t):
        picks = cz[pl.ds(t * PD + perm_s[n], 1), :]
        table = cT[n]
        for b in range(FRAME // 256):
            row = picks[:, b * 256 : (b + 1) * 256]
            hot = jnp.where(iota((SD, 256), 0) == row, 1.0, 0.0).astype(BF16)
            got = nn(table, hot).astype(BF16)
            if b == 0:
                eL[n, t] = got[:, 0:MARGIN]
                own[n, :, 0:128] = got[:, MARGIN:256]
            elif b == 1:
                own[n, :, 128:384] = got
            else:
                own[n, :, 384:512] = got[:, 0:MARGIN]
                eR[n, t] = got[:, MARGIN:256]
        to_left, to_right = halo(n, t)
        to_left.start()
        to_right.start()

    def step(n, t):
        to_left, to_right = halo(n, t)
        to_left.wait_recv()
        to_right.wait_recv()
        at = t * PD + perm_s[n]
        d = dref[pl.ds(at, 1), :]
        e = eref[pl.ds(at, 1), :]
        lane = iota((1, 128), 1)
        a = anc_s[n]
        center, persist, spread, prec = vm_s[a], vp_s[a], vs_s[a], op_s[a]
        front = jnp.where(
            lane < d, hL[n, t].astype(F32), own[n, :, 0:128].astype(F32)
        ).astype(BF16)
        back = jnp.where(
            lane + 384 >= e, hR[n, t].astype(F32), own[n, :, 384:512].astype(F32)
        ).astype(BF16)
        own[n, :, 0:128] = front
        own[n, :, 384:512] = back
        mat = mT[n]
        y = yb[t]
        y = jnp.concatenate([y, y], axis=1)
        weights = []
        for b in range(2):
            cols = slice(b * 256, (b + 1) * 256)
            x = own[n, :, cols]
            vol = x[K:EXT].astype(F32)[0:1]
            h = center + persist * (vol - center) + spread * vn[pl.ds(t, 1), cols]
            drift = nn(mat, x[0:K])
            cloud = (drift + jnp.exp(0.5 * h) * nT[t, :, cols].astype(F32)).astype(BF16)
            hb = h.astype(BF16)
            cT[n, 0:K, cols] = cloud
            cT[n, K:EXT, cols] = jnp.broadcast_to(h, (EXT - K, 256)).astype(BF16)
            vf[pl.ds(n, 1), cols] = hb.astype(F32)
            miss = y - nn(lT[...], cloud)
            ssq = jnp.sum(miss * miss, axis=0, keepdims=True)
            weights.append(-0.5 * prec * ssq)
        logw = jnp.concatenate(weights, axis=1)
        logw = logw + 0.5 * M * jnp.log(jnp.full((1, 1), prec, F32))
        peak = jnp.max(logw, axis=1, keepdims=True)
        mass = jnp.sum(jnp.exp(logw - peak), axis=1, keepdims=True)
        here = lane == t
        stats[pl.ds(n, 1), :] = jnp.where(here, peak, stats[pl.ds(n, 1), :])
        stats[pl.ds(PD + n, 1), :] = jnp.where(here, mass, stats[pl.ds(PD + n, 1), :])

    def both(fn, r, *rest):
        for side in range(2):
            fn(2 * r + side, *rest)

    def wave(r, _):
        @pl.when(r < KEEP)
        def _():
            both(build, r)
            both(draw, r, 0)

        @pl.when(r > 0)
        def _():
            both(step, r - 1, 1)
            both(draw, r - 1, 2)

        @pl.when(r < KEEP)
        def _():
            both(step, r, 0)
            both(draw, r, 1)

        @pl.when(r > 0)
        def _():
            both(step, r - 1, 2)

        return 0

    each_in = ((g > 0, 0), (g < TN - 1, 1))
    for cond, d in each_in:
        @pl.when(cond)
        def _(d=d):
            send_vol(d).wait_recv()

    lax.fori_loop(0, KEEP + 1, wave, 0)

    def join(buf, here):
        order = [buf[(here + 8 - k) % 8] for k in range(8)]
        peak = order[0][0:PD]
        for x in order[1:]:
            peak = jnp.maximum(peak, x[0:PD])
        mass = jnp.zeros((PD, 128), F32)
        for x in order:
            mass = mass + x[PD:] * jnp.exp(x[0:PD] - peak)
        return peak, mass

    s1[0] = stats[...]
    for o in range(1, WN):
        group1(o, stats, s1, 2).start()

    def emit(i, _):
        at = pos_s[i]
        for b in range(2):
            block = cT[at, 0:K, b * 256 : (b + 1) * 256]
            osb[i, b * 256 : (b + 1) * 256, :] = nt(eyer[...], block).astype(BF16)
        pltpu.make_async_copy(osb.at[i], o_states.at[i], out_sem.at[i]).start()
        tmp[pl.ds(i, 1), :] = vf[pl.ds(at, 1), :]
        return 0

    lax.fori_loop(0, PD // 2, emit, 0)
    for o in range(1, WN):
        group1(o, stats, s1, 2).wait_recv()
    peak, mass = join(s1, w)
    s2[0, 0:PD, :] = peak
    s2[0, PD:, :] = mass
    for o in range(1, 8):
        group2(o, s2.at[0], s2, 3).start()
    lax.fori_loop(PD // 2, PD, emit, 0)
    o_vol[...] = tmp[...].astype(BF16)
    for o in range(1, 8):
        group2(o, s2.at[0], s2, 3).wait_recv()
    peak, mass = join(s2, z)
    live = lane8 < STEPS
    part = peak + jnp.log(jnp.where(live, mass, 1.0)) - math.log(SD * JN)
    total = jnp.sum(jnp.where(live, part, 0.0), axis=1, keepdims=True)
    s1[0, 0:PD, :] = jnp.broadcast_to(total, (PD, 128))
    lane1 = iota((1, 128), 1)
    out = jnp.zeros((1, 128), F32)
    for i in range(PD):
        value = s1[0, pl.ds(pos_s[i], 1), :] + pr_s[a8[i]]
        out = jnp.where(lane1 == i, value, out)
    o_ll[...] = out

    for o in range(1, WN):
        group1(o, ctile, g1, 0).wait_send()
        group2(o, c2tile, g2, 1).wait_send()
        group1(o, stats, s1, 2).wait_send()
        group2(o, s2.at[0], s2, 3).wait_send()
    each_dir(lambda d: send_vol(d).wait_send())

    def drain(n, _):
        @pl.when(has_out(n))
        def _():
            c, m = send_copy(n)
            c.wait_send()
            m.wait_send()

        def drain_t(t, _):
            to_left, to_right = halo(n, t)
            to_left.wait_send()
            to_right.wait_send()
            return 0

        lax.fori_loop(0, STEPS, drain_t, 0)
        pltpu.make_async_copy(osb.at[n], o_states.at[n], out_sem.at[n]).wait()
        return 0

    lax.fori_loop(0, PD, drain, 0)


def local(
    states, log_vol, transition, loading, yields, state_noise, vol_noise,
    vol_mean, vol_persist, vol_scale, obs_prec, prior_loglik,
    ancestors, counts, local_anc,
):
    smem = pl.BlockSpec(memory_space=pltpu.SMEM)
    vmem = pl.BlockSpec(memory_space=pltpu.VMEM)
    hbm = pl.BlockSpec(memory_space=pl.ANY)
    dma = pltpu.SemaphoreType.DMA
    v, s = pltpu.VMEM, pltpu.SMEM
    final, vol, ll = pl.pallas_call(
        kernel,
        out_shape=(
            jax.ShapeDtypeStruct((PD, SD, K), BF16),
            jax.ShapeDtypeStruct((PD, SD), BF16),
            jax.ShapeDtypeStruct((1, 128), F32),
        ),
        in_specs=[smem] * 7 + [vmem] * 5 + [hbm] * 3,
        out_specs=(hbm, vmem, vmem),
        scratch_shapes=[
            v((PD, SD, K), BF16), v((PD, K, K), BF16), v((STEPS, SD, K), BF16),
            v((PD, SD, K), BF16), v((PD, K, K), BF16), v((2, PD, SD), F32),
            v((PD, SD, K), BF16), v((PD, K, K), BF16), v((2, PD, SD), F32),
            v((PD, EXT, SD), BF16), v((PD, EXT, SD), BF16), v((PD, K, K), BF16),
            v((STEPS, K, SD), BF16), v((M, K), BF16), v((STEPS, M, M), F32),
            v((PD, STEPS, EXT, MARGIN), BF16), v((PD, STEPS, EXT, MARGIN), BF16),
            v((PD, STEPS, EXT, MARGIN), BF16), v((PD, STEPS, EXT, MARGIN), BF16),
            v((PD, 128), I32), v((PD, 128), I32),
            v((8, PD, 128), I32), v((8, PD, 128), I32),
            v((STEPS * PD, 128), I32), v((STEPS * PD, 128), I32),
            v((STEPS * PD, FRAME), I32),
            v((2 * PD, 128), F32), v((8, 2 * PD, 128), F32), v((8, 2 * PD, 128), F32),
            v((PD, SD), F32), v((PD, SD), F32), v((PD, SD, K), BF16),
            v((PD, SD), F32), v((K, K), BF16),
            s((PD,), I32), s((PD,), I32), s((PD,), I32), s((PD,), I32),
            s((PD,), I32), s((PD,), I32),
            dma((3,)), dma((2, PD)), dma((2, PD)), dma((2,)), dma((2,)),
            dma((2, PD, STEPS)), dma((2, PD, STEPS)),
            dma((4, 8)), dma((4, 8)), dma((PD,)),
        ],
        compiler_params=pltpu.CompilerParams(
            collective_id=0, has_side_effects=True, vmem_limit_bytes=60 << 20
        ),
    )(
        ancestors, counts.reshape(STEPS * PD),
        vol_mean, vol_persist, vol_scale, obs_prec, prior_loglik,
        log_vol, loading, yields, vol_noise, local_anc.reshape(STEPS * PD, FRAME),
        states, transition, state_noise,
    )
    return final, vol, ll[0, :PD]


def solution(mesh):
    placed = (
        P("theta", "state", None),
        P("theta", "state"),
        P("theta", None, None),
        P(),
        P(),
        P(None, "state", None),
        P(None, "state"),
        P(),
        P(),
        P(),
        P(),
        P(),
        P(),
        P(None, "theta", "state"),
        P(None, "theta", "state"),
    )
    return jax.shard_map(
        local,
        mesh=mesh,
        in_specs=placed,
        out_specs=(P("theta", "state", None), P("theta", "state"), P("theta")),
        check_vma=False,
    )
```

time: 282 us -> 84.8 us (0.30)
  local copies, waits for them, and re-layouts: 113 us -> 5.4 us
  starting transfers between devices: 79.6 us -> 0 us
  Pallas kernels: 0 us -> 77.9 us
  matrix products: 38.4 us -> 0 us
  waiting for transfers between devices: 33.5 us -> 0 us
  other arithmetic: 14.5 us -> 0.7 us
    gather x16 -> x0, local copies, waits for them, and re-layouts: 106 us -> none  [the longest x6 75.9 us: local(): jnp.take_along_axis(chosen, jnp.clip(relative, 0, shard_slots - 1), axis=1)]
    pallas_call x0 -> x1, Pallas kernels: none -> 77.9 us  [local(): pl.pallas_call(kernel, out_shape=(jax.ShapeDtypeStruct((PD, SD, K), BF16)...]
    ppermute x16 -> x0, starting transfers between devices: 40.9 us -> none  [the longest x8 24.9 us: padded(): lax.ppermute(lax.slice_in_dim(block, block.shape[dim] - width, None, axis...]
    all_to_all x2 -> x0, starting transfers between devices: 38.7 us -> none  [sent_to_all(): return lax.all_to_all(copies, axis, split_axis=0, concat_axis=0, tiled=True)]
    dot_general x15 -> x0, matrix products: 38.4 us -> none  [the longest x3 16 us: local(): jnp.einsum('psk,pkl->psl', cloud, matrix, preferred_element_type=jnp.floa...]
    ppermute x16 -> x0, waiting for transfers between devices: 21.1 us -> none  [the longest x8 18.7 us: padded(): lax.ppermute(lax.slice_in_dim(block, 0, width, axis=dim), axis, backward)]
    all_to_all x2 -> x0, waiting for transfers between devices: 12.4 us -> none  [sent_to_all(): return lax.all_to_all(copies, axis, split_axis=0, concat_axis=0, tiled=True)]
    concatenate x8 -> x0, other arithmetic: 7.74 us -> none  [the longest x2 7.72 us: padded(): block = jnp.concatenate([low, block, high], axis=dim)]
  transfers between devices with their start and end apart: 18 -> 0, of which waited for: 8 -> 0; matrix products, arithmetic and copies ran while one was open for 47% -> 0% of each run, Pallas kernels for 0% -> 0%
where the time goes in v1:
time: 84.8 us; the launch traced here: 84.6 us
  Pallas kernels  77.9 us (92%)
  local copies, waits for them, and re-layouts  5.4 us (6%)
    pallas_call x1, Pallas kernels, local(): pl.pallas_call(kernel, out_shape=(jax.ShapeDtypeStruct((PD, SD, K), BF16)...  77.9 us
    unnamed x4, local copies, waits for them, and re-layouts  3.66 us

profile of v1, /device:TPU:1, one launch (start us, length us, event | category | flops | bytes accessed | tf_op | source)
XLA Modules:
  0.0 84.6 jit_solution(8531041439384184259)
XLA Ops:
  0.6 0.7 reduce
  1.3 0.6 reshape.12.cnt
  1.9 77.9 %shard_map.166 = (bf16[8,512,256]{2,1,0:T(8,128)(2,1)}, bf16[8,512]{1,0:T(8,128)(2,1)}, f32[1,128]{1,0:T(1,128)}) custom-call(s32[32]{0:T(128)} %anc.1, s32[24]{0:T(128)} %reshape.12.cnt, f32[32]{0:T(128)} %vm_s.1, f32[32]{0:T(128)} %vp_s.1, f32[32]{0:T(128)} %vs_s.1, f32[32]{0:T(128)} %op_s.1, f32[32]{0:T(128)} %pr_s.1, bf16[8,512]{1,0:T(8,128)(2,1)} %lv.1, ...), custom_call_target="tpu_custom_call" | custom-call | tf_op jit(solution)/shard_map/pallas_call | solution.py:473
  79.8 1.1 %slice_bitcast_fusion = f32[8]{0:T(128)} fusion(f32[1,128]{1,0:T(1,128)} %get-tuple-element.8), kind=kLoop, calls=%fused_computation | loop fusion | bytes 64 | tf_op jit(solution)/shard_map/squeeze | solution.py:512
  80.9 0.0 copy-start
  80.9 3.1 %copy.20 = bf16[8,512,256]{2,1,0:T(8,128)(2,1)} copy(bf16[8,512,256]{2,1,0:T(8,128)(2,1)} %get-tuple-element.12) | data formatting | bytes 4194304
  84.0 0.0 copy-done
  84.0 0.6 copy.21
Async XLA Ops:
  80.9 3.1 %copy-start = (bf16[8,512]{1,0:T(8,128)(2,1)S(1)}, bf16[8,512]{1,0:T(8,128)(2,1)}, u32[]{:S(2)}) copy-start(bf16[8,512]{1,0:T(8,128)(2,1)} %get-tuple-element.13) | copy-start | bytes 24580

commit v2 on v1

v2 whole, which is shorter than its diff:
```python
import math

import jax
import jax.numpy as jnp
from jax import lax
from jax.experimental import pallas as pl
from jax.experimental.pallas import tpu as pltpu
from jax.sharding import PartitionSpec as P

K = 256
M = 128
PD = 8
SD = 512
STEPS = 3
MARGIN = 128
FRAME = SD + 2 * MARGIN
EXT = K + 16
HALF = K // 2
KEEP = 4
LAST = 2 * KEEP - 2
TN = 4
JN = 64
WN = 8
BUILD, GO, END, SERVE, PASS = range(5)
ORDER = (
    (BUILD, 0, 0), (SERVE, 0, 0), (GO, 0, 0), (BUILD, 1, 0), (PASS, 0, 0),
    (GO, 0, 1), (GO, 1, 0), (BUILD, 2, 0), (END, 0, 2), (GO, 1, 1),
    (GO, 2, 0), (GO, 3, 0), (END, 1, 2), (GO, 2, 1), (GO, 3, 1),
    (END, 2, 2), (END, 3, 2),
)
PACKED = [
    sum((16 * k + 4 * r + t) << (7 * i) for i, (k, r, t) in enumerate(ORDER[at : at + 4]))
    for at in range(0, len(ORDER), 4)
]
F32 = jnp.float32
BF16 = jnp.bfloat16
I32 = jnp.int32
MESH = pl.DeviceIdType.MESH


def nt(a, b):
    return lax.dot_general(a, b, (((1,), (1,)), ((), ())), preferred_element_type=F32)


def nn(a, b):
    return lax.dot_general(a, b, (((1,), (0,)), ((), ())), preferred_element_type=F32)


def iota(shape, dim):
    return lax.broadcasted_iota(I32, shape, dim)


def eye(n):
    return jnp.where(iota((n, n), 0) == iota((n, n), 1), 1.0, 0.0).astype(BF16)


def kernel(
    anc, vm_s, vp_s, vs_s, op_s, pr_s,
    cnt, lv, ld, yl, vn, la, states, trans, noise,
    o_states, o_vol, o_ll, o_pos,
    st, tr, nz, sc, sm, sv, rc, rm, rv, rcT, req, reqin,
    cT, own, mT, nT, lT, yb, eL, eR, hL, hR,
    ctile, c2tile, g1, g2, dref, eref, cz, stats, s1, s2, lvf, osb, eyer, lines,
    perm_s, src_s, rem_s, anc_s, snd_s,
    ld_sem, th_ss, th_rs, rq_ss, rq_rs, fw_ss, fw_rs, tv_ss, tv_rs, hl_ss, hl_rs, g_ss, g_rs, out_sem,
):
    g = lax.axis_index("theta")
    j = lax.axis_index("state")
    z, w, core = j // WN, j % WN, j % 2
    left, right = (j + JN - 1) % JN, (j + 1) % JN

    def dev(theta, state):
        return {"theta": theta, "state": state}

    barrier = pltpu.get_barrier_semaphore()

    def greet(theta, state):
        pl.semaphore_signal(
            barrier, inc=1, device_id=dev(theta, state), device_id_type=MESH
        )

    for o in range(1, 8):
        greet(g, ((z + o) % 8) * WN + w)
    for o in range(1, WN):
        greet(g, z * WN + (w + o) % WN)
    greet(g, left)
    greet(g, right)

    @pl.when(g > 0)
    def _():
        greet(g - 1, j)

    @pl.when(g < TN - 1)
    def _():
        greet(g + 1, j)

    load_st = pltpu.make_async_copy(states, st, ld_sem.at[0])
    load_tr = pltpu.make_async_copy(trans, tr, ld_sem.at[1])
    load_nz = pltpu.make_async_copy(noise, nz, ld_sem.at[2])
    load_st.start()
    load_tr.start()
    load_nz.start()

    a8 = [anc[g * PD + i] for i in range(PD)]
    off = [lax.shift_right_arithmetic(a, 3) - g for a in a8]
    below = [jnp.where(o == -1, 1, 0) for o in off]
    above = [jnp.where(o == 1, 1, 0) for o in off]
    nb, na, nl = 0, 0, 0
    rank_b, rank_a, rank_l = [], [], []
    for i in range(PD):
        rank_b.append(nb)
        rank_a.append(na)
        rank_l.append(nl)
        nb = nb + below[i]
        na = na + above[i]
        nl = nl + 1 - below[i] - above[i]
    free_b = KEEP - nb
    pos = []
    for i in range(PD):
        l = rank_l[i]
        home = jnp.where(l < free_b, 2 * (nb + l), 2 * (na + l - free_b) + 1)
        slot = jnp.where(
            below[i] == 1,
            2 * rank_b[i],
            jnp.where(above[i] == 1, 2 * rank_a[i] + 1, home),
        )
        pos.append(jnp.clip(slot, 0, PD - 1))
        o_pos[i] = pos[i]
    for n in range(PD):
        who, a = 0, 0
        for i in range(PD):
            hit = pos[i] == n
            who = jnp.where(hit, i, who)
            a = jnp.where(hit, a8[i], a)
        perm_s[n] = who
        anc_s[n] = a
        src_s[n] = a & (PD - 1)
        rem_s[n] = jnp.where(lax.shift_right_arithmetic(a, 3) == g, 0, 1)
    for d, peer in ((0, jnp.minimum(g + 1, TN - 1)), (1, jnp.maximum(g - 1, 0))):
        rank = 0
        chosen = [0] * KEEP
        for i in range(PD):
            a = anc[peer * PD + i]
            hit = jnp.where(lax.shift_right_arithmetic(a, 3) == g, 1, 0)
            for k in range(KEEP):
                take = jnp.where(rank == k, hit, 0)
                chosen[k] = jnp.where(take == 1, a & (PD - 1), chosen[k])
            rank = rank + hit
        for k in range(KEEP):
            snd_s[2 * k + d] = chosen[k]

    lane8 = iota((PD, 128), 1)
    tile = jnp.zeros((PD, 128), I32)
    for t in range(STEPS):
        line = jnp.broadcast_to(cnt[t].astype(F32), (PD, PD))
        line = jnp.where(iota((PD, PD), 0) == iota((PD, PD), 1), line, 0.0)
        column = jnp.sum(line, axis=1, keepdims=True).astype(I32)
        tile = jnp.where(lane8 == t, jnp.broadcast_to(column, (PD, 128)), tile)
    ctile[...] = tile
    lvf[...] = lv[...].astype(F32)
    for d in range(2):
        for k in range(KEEP):
            row = lvf[pl.ds(snd_s[2 * k + d], 1), :]
            sv[d, k : k + 1, :] = row
            sv[d, KEEP + k : KEEP + k + 1, :] = row
    load_st.wait()
    load_tr.wait()

    def fill(n, _):
        s = snd_s[n]
        sc[n] = st[s]
        sm[n] = tr[s, pl.ds(pl.multiple_of(core * HALF, HALF), HALF), :]
        return 0

    def send_copy(n):
        peer = jnp.where(n % 2 == 0, g + 1, g - 1)
        return pltpu.make_async_remote_copy(
            sc.at[n], rc.at[n], th_ss.at[0, n], th_rs.at[0, n],
            device_id=dev(peer, j), device_id_type=MESH,
        )

    def send_mat(n):
        peer = jnp.where(n % 2 == 0, g + 1, g - 1)
        return pltpu.make_async_remote_copy(
            sm.at[n], rm.at[n, core], th_ss.at[1, n], th_rs.at[1, n],
            device_id=dev(peer, j), device_id_type=MESH,
        )

    def forward(n):
        return pltpu.make_async_remote_copy(
            rm.at[n, core], rm.at[n, core], fw_ss.at[n], fw_rs.at[n],
            device_id=dev(g, j + 1 - 2 * core), device_id_type=MESH,
        )

    def pass_on(n):
        @pl.when(has_in(n))
        def _():
            send_mat(n).wait_recv()
            forward(n).start()

    def send_vol(d):
        peer = jnp.where(d == 0, g + 1, g - 1)
        return pltpu.make_async_remote_copy(
            sv.at[d], rv.at[d], tv_ss.at[d], tv_rs.at[d],
            device_id=dev(peer, j), device_id_type=MESH,
        )

    def group1(o, src, dst, u):
        return pltpu.make_async_remote_copy(
            src, dst.at[o], g_ss.at[u, o], g_rs.at[u, o],
            device_id=dev(g, z * WN + (w + o) % WN), device_id_type=MESH,
        )

    def group2(o, src, dst, u):
        return pltpu.make_async_remote_copy(
            src, dst.at[o], g_ss.at[u, o], g_rs.at[u, o],
            device_id=dev(g, ((z + o) % 8) * WN + w), device_id_type=MESH,
        )

    lax.fori_loop(0, 4, fill, 0)
    pl.semaphore_wait(
        barrier, 16 + jnp.where(g > 0, 1, 0) + jnp.where(g < TN - 1, 1, 0)
    )
    for o in range(1, WN):
        group1(o, ctile, g1, 0).start()

    def each_dir(fn):
        @pl.when(g < TN - 1)
        def _():
            fn(0)

        @pl.when(g > 0)
        def _():
            fn(1)

    def has_in(n):
        return jnp.where(n % 2 == 0, g > 0, g < TN - 1)

    def has_out(n):
        return jnp.where(n % 2 == 0, g < TN - 1, g > 0)

    each_dir(lambda d: send_vol(d).start())

    def start_mat(n, _):
        @pl.when(has_out(n))
        def _():
            send_mat(n).start()

        return 0

    def start_copy(n, _):
        @pl.when(has_out(n))
        def _():
            send_copy(n).start()

        return 0

    lax.fori_loop(0, 4, start_mat, 0)
    lax.fori_loop(0, 2, start_copy, 0)
    lax.fori_loop(4, 2 * KEEP, fill, 0)

    def start_more(r, _):
        for d in range(2):
            start_mat(2 * r + 2 + d, 0)
        for d in range(2):
            start_copy(2 * r + d, 0)
        return 0

    lax.fori_loop(1, KEEP - 1, start_more, 0)

    def request(side):
        return pltpu.make_async_remote_copy(
            req.at[side], reqin.at[side], rq_ss.at[side], rq_rs.at[side],
            device_id=dev(g - 1 if side == 0 else g + 1, j), device_id_type=MESH,
        )

    def request_any(d):
        return pltpu.make_async_remote_copy(
            req.at[d], reqin.at[d], rq_ss.at[d], rq_rs.at[d],
            device_id=dev(jnp.where(d == 0, g - 1, g + 1), j), device_id_type=MESH,
        )

    def send_drawn(d):
        return pltpu.make_async_remote_copy(
            own.at[PD + d], rcT.at[d], th_ss.at[0, LAST + d], th_rs.at[0, LAST + d],
            device_id=dev(jnp.where(d == 0, g + 1, g - 1), j), device_id_type=MESH,
        )

    takes = (g > 0, g < TN - 1)
    gives = (g < TN - 1, g > 0)

    eyer[...] = eye(K)
    lines[...] = iota((256, 256), 0).astype(F32).astype(BF16)
    load_nz.wait()
    for t in range(STEPS):
        nT[t] = nt(eyer[...], nz[t]).astype(BF16)
        yb[t] = jnp.transpose(jnp.broadcast_to(yl[t : t + 1, :], (M, M)))
    lT[...] = nt(eye(M), ld[...]).astype(BF16)
    stats[...] = jnp.zeros_like(stats)

    before = jnp.zeros((PD, 128), I32)
    whole = ctile[...]
    for o in range(1, WN):
        group1(o, ctile, g1, 0).wait_recv()
        got = g1[o]
        source = (w + WN - o) % WN
        before = before + jnp.where(source < w, got, 0)
        whole = whole + got
    c2tile[...] = whole
    for o in range(1, 8):
        group2(o, c2tile, g2, 1).start()
    for o in range(1, 8):
        group2(o, c2tile, g2, 1).wait_recv()
        source = (z + 8 - o) % 8
        before = before + jnp.where(source < z, g2[o], 0)
    first = before - SD * j
    for t in range(STEPS):
        d = jnp.broadcast_to(first[:, t : t + 1], (PD, 128))
        e = d + jnp.broadcast_to(tile[:, t : t + 1], (PD, 128))
        dref[t * PD : (t + 1) * PD, :] = d
        eref[t * PD : (t + 1) * PD, :] = e
        shift = jnp.concatenate([d + MARGIN] * (FRAME // 128), axis=1)
        x = la[t * PD : (t + 1) * PD, :]
        for b in range(9):
            x = jnp.where((shift & (1 << b)) != 0, pltpu.roll(x, 1 << b, 1), x)
        cz[t * PD : (t + 1) * PD, :] = x

    def halo(n, t):
        to_left = pltpu.make_async_remote_copy(
            eL.at[n, t], hR.at[n, t], hl_ss.at[0, n, t], hl_rs.at[0, n, t],
            device_id=dev(g, left), device_id_type=MESH,
        )
        to_right = pltpu.make_async_remote_copy(
            eR.at[n, t], hL.at[n, t], hl_ss.at[1, n, t], hl_rs.at[1, n, t],
            device_id=dev(g, right), device_id_type=MESH,
        )
        return to_left, to_right

    def arrive(n):
        @pl.when(has_in(n))
        def _():
            send_copy(n).wait_recv()
            forward(n).wait_recv()

        pass_on(n + 2)

    def put_cloud(n, cloud, vol):
        cT[n, 0:K, :] = nt(eyer[...], cloud).astype(BF16)
        cT[n, K:EXT, :] = jnp.broadcast_to(vol, (EXT - K, SD)).astype(BF16)

    def build_mat(n):
        got = jnp.concatenate([rm[n, 0], rm[n, 1]], axis=0).astype(F32)
        mat = jnp.where(rem_s[n] == 1, got, tr[src_s[n]].astype(F32)).astype(BF16)
        mT[n] = nt(eyer[...], mat).astype(BF16)

    def build(n):
        src = src_s[n]
        remote = rem_s[n] == 1
        cloud = jnp.where(remote, rc[n].astype(F32), st[src].astype(F32)).astype(BF16)
        got = rv[n % 2, pl.ds(n // 2, 1), :]
        put_cloud(n, cloud, jnp.where(remote, got, lvf[pl.ds(src, 1), :]))
        build_mat(n)

    def row_of(n, t):
        return jnp.where(n < PD, t * PD + perm_s[jnp.minimum(n, PD - 1)], STEPS * PD + n - PD)

    def picks_of(n, t):
        return cz[pl.ds(row_of(n, t), 1), :]

    def draw(ns, t, tables):
        rows = lines[...]
        picks = [picks_of(n, t).astype(F32) for n in ns]
        out = []
        for b in range(FRAME // 256):
            hots = []
            for pick in picks:
                row = pick[:, b * 256 : (b + 1) * 256]
                hots.append(
                    jnp.concatenate(
                        [
                            jnp.where(
                                rows == (row - float(part * 256)).astype(BF16),
                                jnp.ones((), BF16),
                                jnp.zeros((), BF16),
                            )
                            for part in range(2)
                        ],
                        axis=0,
                    )
                )
            out.append([nn(x, hot).astype(BF16) for x, hot in zip(tables, hots)])
        for i, n in enumerate(ns):
            eL[n, t] = out[0][i][:, 0:MARGIN]
            eR[n, t] = out[2][i][:, MARGIN:256]
        for i, n in enumerate(ns):
            own[n, :, 0:128] = out[0][i][:, MARGIN:256]
            own[n, :, 128:384] = out[1][i]
            own[n, :, 384:512] = out[2][i][:, 0:MARGIN]

    def send_halo(n, t):
        for copy in halo(n, t):
            copy.start()

    def wait_halo(n, t):
        for copy in halo(n, t):
            copy.wait_recv()

    def merge_with(n, t, d, e):
        lane = iota((1, 128), 1)
        front = jnp.where(
            lane < d, hL[n, t].astype(F32), own[n, :, 0:128].astype(F32)
        ).astype(BF16)
        back = jnp.where(
            lane + 384 >= e, hR[n, t].astype(F32), own[n, :, 384:512].astype(F32)
        ).astype(BF16)
        own[n, :, 0:128] = front
        own[n, :, 384:512] = back

    def merge(n, t):
        at = row_of(n, t)
        merge_with(n, t, dref[pl.ds(at, 1), :], eref[pl.ds(at, 1), :])

    def step(ns, t):
        lane = iota((1, 128), 1)
        halves = [slice(b * 256, (b + 1) * 256) for b in range(2)]
        xs = [[own[n, :, c] for c in halves] for n in ns]
        mats = [mT[n] for n in ns]
        noise_t = [nT[t, :, c].astype(F32) for c in halves]
        shocks = [vn[pl.ds(t, 1), c] for c in halves]
        y = yb[t]
        y = jnp.concatenate([y, y], axis=1)
        load = lT[...]
        clouds, hs = [], []
        for n, x, mat in zip(ns, xs, mats):
            a = anc_s[n]
            center, persist, spread = vm_s[a], vp_s[a], vs_s[a]
            cloud, level = [], []
            for b in range(2):
                vol = x[b][K:EXT].astype(F32)[0:1]
                h = center + persist * (vol - center) + spread * shocks[b]
                drift = nn(mat, x[b][0:K])
                cloud.append((drift + jnp.exp(0.5 * h) * noise_t[b]).astype(BF16))
                level.append(h)
            clouds.append(cloud)
            hs.append(level)
        tables = []
        for n, cloud, level in zip(ns, clouds, hs):
            h = jnp.concatenate(level, axis=1)
            cT[n, 0:K, 0:256] = cloud[0]
            cT[n, 0:K, 256:512] = cloud[1]
            o_vol[pl.ds(n, 1), :] = h.astype(BF16).astype(F32)
            wide = jnp.broadcast_to(h, (EXT - K, SD)).astype(BF16)
            tables.append(
                jnp.concatenate([jnp.concatenate(cloud, axis=1), wide], axis=0)
            )

        def weigh():
            for n, cloud in zip(ns, clouds):
                prec = op_s[anc_s[n]]
                parts = []
                for b in range(2):
                    miss = y - nn(load, cloud[b])
                    ssq = jnp.sum(miss * miss, axis=0, keepdims=True)
                    parts.append(-0.5 * prec * ssq)
                logw = jnp.concatenate(parts, axis=1)
                logw = logw + 0.5 * M * jnp.log(jnp.full((1, 1), prec, F32))
                peak = jnp.max(logw, axis=1, keepdims=True)
                mass = jnp.sum(jnp.exp(logw - peak), axis=1, keepdims=True)
                here = lane == t
                for at, value in ((n, peak), (PD + n, mass)):
                    old = stats[pl.ds(at, 1), :]
                    stats[pl.ds(at, 1), :] = jnp.where(here, value, old)

        return tables, weigh

    def finish(n):
        for b in range(2):
            block = cT[n, 0:K, b * 256 : (b + 1) * 256]
            osb[n, b * 256 : (b + 1) * 256, :] = nt(eyer[...], block).astype(BF16)
        pltpu.make_async_copy(osb.at[n], o_states.at[n], out_sem.at[n]).start()

    def ask():
        for side in range(2):
            n = LAST + side
            row = picks_of(n, 0)
            for b in range(FRAME // 128):
                req[side, b : b + 1, :] = row[:, b * 128 : (b + 1) * 128]
            req[side, 6:7, :] = dref[pl.ds(perm_s[n], 1), :]
            req[side, 7:8, :] = eref[pl.ds(perm_s[n], 1), :]
        for side in range(2):
            @pl.when(takes[side])
            def _(side=side):
                request(side).start()

        for side in range(2):
            src = src_s[LAST + side]
            put_cloud(LAST + side, st[src], lvf[pl.ds(src, 1), :])
        draw((LAST, LAST + 1), 0, [cT[LAST], cT[LAST + 1]])
        send_halo(LAST, 0)
        send_halo(LAST + 1, 0)

    def take_request(d):
        @pl.when(gives[d])
        def _():
            request_any(d).wait_recv()

        at = STEPS * PD + d
        cz[pl.ds(at, 1), :] = jnp.concatenate(
            [reqin[d, b : b + 1, :] for b in range(FRAME // 128)], axis=1
        )
        dref[pl.ds(at, 1), :] = reqin[d, 6:7, :]
        eref[pl.ds(at, 1), :] = reqin[d, 7:8, :]

    def task(m, _):
        code = PACKED[0]
        for k in range(1, len(PACKED)):
            code = jnp.where(m // 4 == k, PACKED[k], code)
        code = lax.shift_right_logical(code, 7 * (m % 4)) & 127
        kind, r, t = code // 16, (code // 4) % 4, code % 4
        pair = (2 * r, 2 * r + 1)
        late = (r == KEEP - 1) & (t == 0)

        @pl.when(kind == BUILD)
        def _():
            for n in pair:
                arrive(n)
            for n in pair:
                build(n)
            draw(pair, 0, [cT[n] for n in pair])
            for n in pair:
                send_halo(n, 0)

        @pl.when(kind == SERVE)
        def _():
            for d in range(2):
                take_request(d)
            for d in range(2):
                put_cloud(PD + d, sc[LAST + d], sv[d, KEEP - 1 : KEEP, :])
            draw((PD, PD + 1), 0, [cT[PD], cT[PD + 1]])
            for d in range(2):
                send_halo(PD + d, 0)

        @pl.when(kind == PASS)
        def _():
            for d in range(2):
                wait_halo(PD + d, 0)
            for d in range(2):
                merge(PD + d, 0)
            for d in range(2):
                @pl.when(gives[d])
                def _(d=d):
                    send_drawn(d).start()

            for n in (LAST, LAST + 1):
                wait_halo(n, 0)
            for n in (LAST, LAST + 1):
                merge(n, 0)

        @pl.when((kind == GO) & late)
        def _():
            for side in range(2):
                @pl.when(takes[side])
                def _(side=side):
                    forward(LAST + side).wait_recv()
                    send_drawn(side).wait_recv()

            for side in range(2):
                n = LAST + side
                build_mat(n)
                own[n] = jnp.where(
                    rem_s[n] == 1, rcT[side].astype(F32), own[n].astype(F32)
                ).astype(BF16)

        @pl.when(((kind == GO) | (kind == END)) & jnp.logical_not(late))
        def _():
            for n in pair:
                wait_halo(n, t)
            for n in pair:
                merge(n, t)

        @pl.when(kind == GO)
        def _():
            tables, weigh = step(pair, t)
            draw(pair, t + 1, tables)
            for n in pair:
                send_halo(n, t + 1)
            weigh()

        @pl.when(kind == END)
        def _():
            step(pair, t)[1]()

        @pl.when((kind == END) & (r < 2))
        def _():
            for n in pair:
                finish(n)

        return 0

    each_in = ((g > 0, 0), (g < TN - 1, 1))
    for cond, d in each_in:
        @pl.when(cond)
        def _(d=d):
            send_vol(d).wait_recv()

    ask()
    pass_on(0)
    pass_on(1)
    lax.fori_loop(0, len(ORDER), task, 0)

    def join(buf, here):
        order = [buf[(here + 8 - k) % 8] for k in range(8)]
        peak = order[0][0:PD]
        for x in order[1:]:
            peak = jnp.maximum(peak, x[0:PD])
        mass = jnp.zeros((PD, 128), F32)
        for x in order:
            mass = mass + x[PD:] * jnp.exp(x[0:PD] - peak)
        return peak, mass

    s1[0] = stats[...]
    for o in range(1, WN):
        group1(o, stats, s1, 2).start()

    for n in range(LAST - 2, PD):
        finish(n)
    for o in range(1, WN):
        group1(o, stats, s1, 2).wait_recv()
    peak, mass = join(s1, w)
    s2[0, 0:PD, :] = peak
    s2[0, PD:, :] = mass
    for o in range(1, 8):
        group2(o, s2.at[0], s2, 3).start()
    for o in range(1, 8):
        group2(o, s2.at[0], s2, 3).wait_recv()
    peak, mass = join(s2, z)
    live = lane8 < STEPS
    part = peak + jnp.log(jnp.where(live, mass, 1.0)) - math.log(SD * JN)
    total = jnp.sum(jnp.where(live, part, 0.0), axis=1, keepdims=True)
    o_ll[...] = jnp.broadcast_to(total, (PD, 128))

    for o in range(1, WN):
        group1(o, ctile, g1, 0).wait_send()
        group2(o, c2tile, g2, 1).wait_send()
        group1(o, stats, s1, 2).wait_send()
        group2(o, s2.at[0], s2, 3).wait_send()
    each_dir(lambda d: send_vol(d).wait_send())

    for d in range(2):
        @pl.when(gives[d])
        def _(d=d):
            send_drawn(d).wait_send()

        @pl.when(takes[d])
        def _(d=d):
            request(d).wait_send()

        for copy in halo(PD + d, 0):
            copy.wait_send()

    def drain(n, _):
        @pl.when(has_out(n))
        def _():
            send_mat(n).wait_send()

        @pl.when(has_out(n) & (n < LAST))
        def _():
            send_copy(n).wait_send()

        @pl.when(has_in(n))
        def _():
            forward(n).wait_send()

        def drain_t(t, _):
            to_left, to_right = halo(n, t)
            to_left.wait_send()
            to_right.wait_send()
            return 0

        lax.fori_loop(0, STEPS, drain_t, 0)
        pltpu.make_async_copy(osb.at[n], o_states.at[n], out_sem.at[n]).wait()
        return 0

    lax.fori_loop(0, PD, drain, 0)


def reorder(anc, pos, pr_s, res, vol, ll, o_states, o_vol, o_ll, buf, rows, sem):
    g = lax.axis_index("theta")

    def take(i):
        return pltpu.make_async_copy(res.at[pos[i]], buf.at[i], sem.at[0, i])

    def give(i):
        return pltpu.make_async_copy(buf.at[i], o_states.at[i], sem.at[1, i])

    for i in range(PD):
        take(i).start()
    lane = iota((1, 128), 1)
    out = jnp.zeros((1, 128), F32)
    for i in range(PD):
        rows[i : i + 1, :] = vol[pl.ds(pos[i], 1), :]
        value = ll[pl.ds(pos[i], 1), :] + pr_s[anc[g * PD + i]]
        out = jnp.where(lane == i, value, out)
    o_vol[...] = rows[...].astype(BF16)
    o_ll[...] = out[:, 0:PD]
    for i in range(PD):
        take(i).wait()
        give(i).start()
    for i in range(PD):
        give(i).wait()


def local(
    states, log_vol, transition, loading, yields, state_noise, vol_noise,
    vol_mean, vol_persist, vol_scale, obs_prec, prior_loglik,
    ancestors, counts, local_anc,
):
    smem = pl.BlockSpec(memory_space=pltpu.SMEM)
    vmem = pl.BlockSpec(memory_space=pltpu.VMEM)
    hbm = pl.BlockSpec(memory_space=pl.ANY)
    dma = pltpu.SemaphoreType.DMA
    v, s = pltpu.VMEM, pltpu.SMEM
    res, vol, ll, pos = pl.pallas_call(
        kernel,
        out_shape=(
            jax.ShapeDtypeStruct((PD, SD, K), BF16),
            jax.ShapeDtypeStruct((PD, SD), F32),
            jax.ShapeDtypeStruct((PD, 128), F32),
            jax.ShapeDtypeStruct((PD,), I32),
        ),
        in_specs=[smem] * 6 + [vmem] * 6 + [hbm] * 3,
        out_specs=(hbm, vmem, vmem, smem),
        scratch_shapes=[
            v((PD, SD, K), BF16), v((PD, K, K), BF16), v((STEPS, SD, K), BF16),
            v((PD, SD, K), BF16), v((PD, HALF, K), BF16), v((2, PD, SD), F32),
            v((PD, SD, K), BF16), v((PD, 2, HALF, K), BF16), v((2, PD, SD), F32),
            v((2, EXT, SD), BF16), v((2, 8, 128), I32), v((2, 8, 128), I32),
            v((PD + 2, EXT, SD), BF16), v((PD + 2, EXT, SD), BF16), v((PD, K, K), BF16),
            v((STEPS, K, SD), BF16), v((M, K), BF16), v((STEPS, M, M), F32),
            v((PD + 2, STEPS, EXT, MARGIN), BF16), v((PD + 2, STEPS, EXT, MARGIN), BF16),
            v((PD + 2, STEPS, EXT, MARGIN), BF16), v((PD + 2, STEPS, EXT, MARGIN), BF16),
            v((PD, 128), I32), v((PD, 128), I32),
            v((8, PD, 128), I32), v((8, PD, 128), I32),
            v((STEPS * PD + 8, 128), I32), v((STEPS * PD + 8, 128), I32),
            v((STEPS * PD + 8, FRAME), I32),
            v((2 * PD, 128), F32), v((8, 2 * PD, 128), F32), v((8, 2 * PD, 128), F32),
            v((PD, SD), F32), v((PD, SD, K), BF16), v((K, K), BF16), v((256, 256), BF16),
            s((PD,), I32), s((PD,), I32), s((PD,), I32), s((PD,), I32), s((PD,), I32),
            dma((3,)), dma((2, PD)), dma((2, PD)), dma((2,)), dma((2,)), dma((PD,)), dma((PD,)),
            dma((2,)), dma((2,)), dma((2, PD + 2, STEPS)), dma((2, PD + 2, STEPS)),
            dma((4, 8)), dma((4, 8)), dma((PD,)),
        ],
        compiler_params=pltpu.CompilerParams(
            collective_id=0, has_side_effects=True, vmem_limit_bytes=63 << 20
        ),
    )(
        ancestors, vol_mean, vol_persist, vol_scale, obs_prec, prior_loglik,
        counts.transpose(0, 2, 1), log_vol, loading, yields, vol_noise,
        local_anc.reshape(STEPS * PD, FRAME), states, transition, state_noise,
    )
    final, final_vol, loglik = pl.pallas_call(
        reorder,
        out_shape=(
            jax.ShapeDtypeStruct((PD, SD, K), BF16),
            jax.ShapeDtypeStruct((PD, SD), BF16),
            jax.ShapeDtypeStruct((1, PD), F32),
        ),
        in_specs=[smem] * 3 + [hbm, vmem, vmem],
        out_specs=(hbm, vmem, vmem),
        scratch_shapes=[v((PD, SD, K), BF16), v((PD, SD), F32), dma((2, PD))],
        compiler_params=pltpu.CompilerParams(vmem_limit_bytes=63 << 20),
    )(ancestors, pos, prior_loglik, res, vol, ll)
    return final, final_vol, loglik.reshape(PD)


def solution(mesh):
    placed = (
        P("theta", "state", None),
        P("theta", "state"),
        P("theta", None, None),
        P(),
        P(),
        P(None, "state", None),
        P(None, "state"),
        P(),
        P(),
        P(),
        P(),
        P(),
        P(),
        P(None, "theta", "state"),
        P(None, "theta", "state"),
    )
    return jax.shard_map(
        local,
        mesh=mesh,
        in_specs=placed,
        out_specs=(P("theta", "state", None), P("theta", "state"), P("theta")),
        check_vma=False,
    )
```

time: 84.8 us -> 81 us (0.955)
  local copies, waits for them, and re-layouts: 5.4 us -> 0 us
  Pallas kernels: 77.9 us -> 80.1 us
    pallas_call x0 -> x1, Pallas kernels: none -> 3.73 us  [local(): pl.pallas_call(reorder, out_shape=(jax.ShapeDtypeStruct((PD, SD, K), BF16...]
    unnamed x4 -> x0, local copies, waits for them, and re-layouts: 3.66 us -> none
    pallas_call x1, Pallas kernels: 77.9 us -> 76.4 us  [local(): pl.pallas_call(kernel, out_shape=(jax.ShapeDtypeStruct((PD, SD, K), BF16)...]
    squeeze x1 -> x0, local copies, waits for them, and re-layouts: 1.14 us -> none  [local(): return (final, vol, ll[0, :PD])]
where the time goes in v2:
time: 81 us; the launch traced here: 80.8 us
  Pallas kernels  80.1 us (99%)
    pallas_call x1, Pallas kernels, local(): pl.pallas_call(kernel, out_shape=(jax.ShapeDtypeStruct((PD, SD, K), BF16)...  76.4 us
    pallas_call x1, Pallas kernels, local(): pl.pallas_call(reorder, out_shape=(jax.ShapeDtypeStruct((PD, SD, K), BF16...  3.73 us

profile of v2, /device:TPU:1, one launch (start us, length us, event | category | flops | bytes accessed | tf_op | source)
XLA Modules:
  0.0 80.8 jit_solution(12556266101824337259)
XLA Ops:
  0.6 76.4 %shard_map.166 = (bf16[8,512,256]{2,1,0:T(8,128)(2,1)}, f32[8,512]{1,0:T(8,128)}, f32[8,128]{1,0:T(8,128)}, s32[8]{0:T(128)}) custom-call(s32[32]{0:T(128)} %anc.3, f32[32]{0:T(128)} %vm_s.1, f32[32]{0:T(128)} %vp_s.1, f32[32]{0:T(128)} %vs_s.1, f32[32]{0:T(128)} %op_s.1, f32[32]{0:T(128)} %pr_s.3, s32[3,1,8]{2,1,0:T(1,128)} %bitcast.4, bf16[8,512]{1,0:T(8,128)(2,1)} %lv.1, ...), custom_call_target="tpu_custom_call" | custom-call | tf_op jit(solution)/shard_map/pallas_call | solution.py:723
  77.0 3.7 %shard_map.167 = (bf16[8,512,256]{2,1,0:T(8,128)(2,1)}, bf16[8,512]{1,0:T(8,128)(2,1)}, f32[1,8]{1,0:T(1,128)}) custom-call(s32[32]{0:T(128)} %anc.3, s32[8]{0:T(128)} %get-tuple-element.10.pos, f32[32]{0:T(128)} %pr_s.3, bf16[8,512,256]{2,1,0:T(8,128)(2,1)} %get-tuple-element.11.res, f32[8,512]{1,0:T(8,128)} %get-tuple-element.12.vol, ...), custom_call_target="tpu_custom_call" | custom-call | tf_op jit(solution)/shard_map/pallas_call | solution.py:761

commit v3 on v2

--- a/solution.py
+++ b/solution.py
@@ -16,6 +16,8 @@
 FRAME = SD + 2 * MARGIN
 EXT = K + 16
 HALF = K // 2
+Q = 2
+ROWS = HALF // Q
 KEEP = 4
 LAST = 2 * KEEP - 2
 TN = 4
@@ -23,10 +25,7 @@
 WN = 8
 BUILD, GO, END, SERVE, PASS = range(5)
 ORDER = (
-    (BUILD, 0, 0), (SERVE, 0, 0), (GO, 0, 0), (BUILD, 1, 0), (PASS, 0, 0),
-    (GO, 0, 1), (GO, 1, 0), (BUILD, 2, 0), (END, 0, 2), (GO, 1, 1),
-    (GO, 2, 0), (GO, 3, 0), (END, 1, 2), (GO, 2, 1), (GO, 3, 1),
-    (END, 2, 2), (END, 3, 2),
+    (BUILD, 0, 0), (GO, 0, 0), (BUILD, 1, 0), (SERVE, 0, 0), (GO, 0, 1), (GO, 1, 0), (PASS, 0, 0), (BUILD, 2, 0), (END, 0, 2), (GO, 1, 1), (GO, 2, 0), (GO, 3, 0), (END, 1, 2), (GO, 2, 1), (GO, 3, 1), (END, 2, 2), (END, 3, 2),
 )
 PACKED = [
     sum((16 * k + 4 * r + t) << (7 * i) for i, (k, r, t) in enumerate(ORDER[at : at + 4]))
@@ -62,11 +61,12 @@
     cT, own, mT, nT, lT, yb, eL, eR, hL, hR,
     ctile, c2tile, g1, g2, dref, eref, cz, stats, s1, s2, lvf, osb, eyer, lines,
     perm_s, src_s, rem_s, anc_s, snd_s,
-    ld_sem, th_ss, th_rs, rq_ss, rq_rs, fw_ss, fw_rs, tv_ss, tv_rs, hl_ss, hl_rs, g_ss, g_rs, out_sem,
+    ld_sem, th_ss, th_rs, rq_ss, rq_rs, zf_ss, zf_rs, fw_ss, fw_rs, tv_ss, tv_rs, hl_ss, hl_rs, g_ss, g_rs, out_sem,
 ):
     g = lax.axis_index("theta")
     j = lax.axis_index("state")
     z, w, core = j // WN, j % WN, j % 2
+    zq = z % Q
     left, right = (j + JN - 1) % JN, (j + 1) % JN
 
     def dev(theta, state):
@@ -169,7 +169,7 @@
     def fill(n, _):
         s = snd_s[n]
         sc[n] = st[s]
-        sm[n] = tr[s, pl.ds(pl.multiple_of(core * HALF, HALF), HALF), :]
+        sm[n] = tr[s, pl.ds(pl.multiple_of(core * HALF + zq * ROWS, ROWS), ROWS), :]
         return 0
 
     def send_copy(n):
@@ -182,7 +182,7 @@
     def send_mat(n):
         peer = jnp.where(n % 2 == 0, g + 1, g - 1)
         return pltpu.make_async_remote_copy(
-            sm.at[n], rm.at[n, core], th_ss.at[1, n], th_rs.at[1, n],
+            sm.at[n], rm.at[n, core, zq], th_ss.at[1, n], th_rs.at[1, n],
             device_id=dev(peer, j), device_id_type=MESH,
         )
 
@@ -192,10 +192,29 @@
             device_id=dev(g, j + 1 - 2 * core), device_id_type=MESH,
         )
 
+    def spread(n, o):
+        return pltpu.make_async_remote_copy(
+            rm.at[n, core, zq], rm.at[n, core, zq], zf_ss.at[n, o], zf_rs.at[n, o],
+            device_id=dev(g, (z - zq + (zq + o) % Q) * WN + w), device_id_type=MESH,
+        )
+
     def pass_on(n):
         @pl.when(has_in(n))
         def _():
             send_mat(n).wait_recv()
+            for o in range(1, Q):
+                spread(n, o).start()
+
+    def pass_two(n):
+        @pl.when(has_in(n))
+        def _():
+            for o in range(1, Q):
+                came = rm.at[n, core, (zq + Q - o) % Q]
+                pltpu.make_async_remote_copy(
+                    came, came, zf_ss.at[n, o], zf_rs.at[n, o],
+                    device_id=dev(g, (z - zq + (zq + o) % Q) * WN + w),
+                    device_id_type=MESH,
+                ).wait_recv()
             forward(n).start()
 
     def send_vol(d):
@@ -340,16 +359,19 @@
         @pl.when(has_in(n))
         def _():
             send_copy(n).wait_recv()
-            forward(n).wait_recv()
-
-        pass_on(n + 2)
+
 
     def put_cloud(n, cloud, vol):
         cT[n, 0:K, :] = nt(eyer[...], cloud).astype(BF16)
         cT[n, K:EXT, :] = jnp.broadcast_to(vol, (EXT - K, SD)).astype(BF16)
 
     def build_mat(n):
-        got = jnp.concatenate([rm[n, 0], rm[n, 1]], axis=0).astype(F32)
+        @pl.when(has_in(n))
+        def _():
+            forward(n).wait_recv()
+
+        pieces = [rm[n, c, q] for c in range(2) for q in range(Q)]
+        got = jnp.concatenate(pieces, axis=0).astype(F32)
         mat = jnp.where(rem_s[n] == 1, got, tr[src_s[n]].astype(F32)).astype(BF16)
         mT[n] = nt(eyer[...], mat).astype(BF16)
 
@@ -359,7 +381,6 @@
         cloud = jnp.where(remote, rc[n].astype(F32), st[src].astype(F32)).astype(BF16)
         got = rv[n % 2, pl.ds(n // 2, 1), :]
         put_cloud(n, cloud, jnp.where(remote, got, lvf[pl.ds(src, 1), :]))
-        build_mat(n)
 
     def row_of(n, t):
         return jnp.where(n < PD, t * PD + perm_s[jnp.minimum(n, PD - 1)], STEPS * PD + n - PD)
@@ -492,12 +513,6 @@
             def _(side=side):
                 request(side).start()
 
-        for side in range(2):
-            src = src_s[LAST + side]
-            put_cloud(LAST + side, st[src], lvf[pl.ds(src, 1), :])
-        draw((LAST, LAST + 1), 0, [cT[LAST], cT[LAST + 1]])
-        send_halo(LAST, 0)
-        send_halo(LAST + 1, 0)
 
     def take_request(d):
         @pl.when(gives[d])
@@ -523,6 +538,10 @@
         @pl.when(kind == BUILD)
         def _():
             for n in pair:
+                pass_two(n)
+            for n in pair:
+                pass_on(n + 2)
+            for n in pair:
                 arrive(n)
             for n in pair:
                 build(n)
@@ -534,6 +553,12 @@
         def _():
             for d in range(2):
                 take_request(d)
+            for side in range(2):
+                src = src_s[LAST + side]
+                put_cloud(LAST + side, st[src], lvf[pl.ds(src, 1), :])
+            draw((LAST, LAST + 1), 0, [cT[LAST], cT[LAST + 1]])
+            send_halo(LAST, 0)
+            send_halo(LAST + 1, 0)
             for d in range(2):
                 put_cloud(PD + d, sc[LAST + d], sv[d, KEEP - 1 : KEEP, :])
             draw((PD, PD + 1), 0, [cT[PD], cT[PD + 1]])
@@ -561,12 +586,10 @@
             for side in range(2):
                 @pl.when(takes[side])
                 def _(side=side):
-                    forward(LAST + side).wait_recv()
                     send_drawn(side).wait_recv()
 
             for side in range(2):
                 n = LAST + side
-                build_mat(n)
                 own[n] = jnp.where(
                     rem_s[n] == 1, rcT[side].astype(F32), own[n].astype(F32)
                 ).astype(BF16)
@@ -577,6 +600,16 @@
                 wait_halo(n, t)
             for n in pair:
                 merge(n, t)
+
+        @pl.when((kind == GO) & (t == 0))
+        def _():
+            for n in pair:
+                build_mat(n)
+
+        @pl.when((kind == GO) & (t == 0) & (r == KEEP - 2))
+        def _():
+            for n in (LAST, LAST + 1):
+                pass_two(n)
 
         @pl.when(kind == GO)
         def _():
@@ -670,6 +703,8 @@
         @pl.when(has_in(n))
         def _():
             forward(n).wait_send()
+            for o in range(1, Q):
+                spread(n, o).wait_send()
 
         def drain_t(t, _):
             to_left, to_right = halo(n, t)
@@ -732,8 +767,8 @@
         out_specs=(hbm, vmem, vmem, smem),
         scratch_shapes=[
             v((PD, SD, K), BF16), v((PD, K, K), BF16), v((STEPS, SD, K), BF16),
-            v((PD, SD, K), BF16), v((PD, HALF, K), BF16), v((2, PD, SD), F32),
-            v((PD, SD, K), BF16), v((PD, 2, HALF, K), BF16), v((2, PD, SD), F32),
+            v((PD, SD, K), BF16), v((PD, ROWS, K), BF16), v((2, PD, SD), F32),
+            v((PD, SD, K), BF16), v((PD, 2, Q, ROWS, K), BF16), v((2, PD, SD), F32),
             v((2, EXT, SD), BF16), v((2, 8, 128), I32), v((2, 8, 128), I32),
             v((PD + 2, EXT, SD), BF16), v((PD + 2, EXT, SD), BF16), v((PD, K, K), BF16),
             v((STEPS, K, SD), BF16), v((M, K), BF16), v((STEPS, M, M), F32),
@@ -746,7 +781,7 @@
             v((2 * PD, 128), F32), v((8, 2 * PD, 128), F32), v((8, 2 * PD, 128), F32),
             v((PD, SD), F32), v((PD, SD, K), BF16), v((K, K), BF16), v((256, 256), BF16),
             s((PD,), I32), s((PD,), I32), s((PD,), I32), s((PD,), I32), s((PD,), I32),
-            dma((3,)), dma((2, PD)), dma((2, PD)), dma((2,)), dma((2,)), dma((PD,)), dma((PD,)),
+            dma((3,)), dma((2, PD)), dma((2, PD)), dma((2,)), dma((2,)), dma((PD, Q)), dma((PD, Q)), dma((PD,)), dma((PD,)),
             dma((2,)), dma((2,)), dma((2, PD + 2, STEPS)), dma((2, PD + 2, STEPS)),
             dma((4, 8)), dma((4, 8)), dma((PD,)),
         ],

time: 81 us -> 76.7 us (0.947)
  Pallas kernels: 80.1 us -> 75.6 us
    pallas_call x1, Pallas kernels: 76.4 us -> 71.9 us  [local(): pl.pallas_call(kernel, out_shape=(jax.ShapeDtypeStruct((PD, SD, K), BF16)...]
where the time goes in v3:
time: 76.7 us; the launch traced here: 76.3 us
  Pallas kernels  75.6 us (99%)
    pallas_call x1, Pallas kernels, local(): pl.pallas_call(kernel, out_shape=(jax.ShapeDtypeStruct((PD, SD, K), BF16)...  71.9 us
    pallas_call x1, Pallas kernels, local(): pl.pallas_call(reorder, out_shape=(jax.ShapeDtypeStruct((PD, SD, K), BF16...  3.73 us

profile of v3, /device:TPU:1, one launch (start us, length us, event | category | flops | bytes accessed | tf_op | source)
XLA Modules:
  0.0 76.3 jit_solution(78849653886779000)
XLA Ops:
  0.6 71.9 %shard_map.166 = (bf16[8,512,256]{2,1,0:T(8,128)(2,1)}, f32[8,512]{1,0:T(8,128)}, f32[8,128]{1,0:T(8,128)}, s32[8]{0:T(128)}) custom-call(s32[32]{0:T(128)} %anc.3, f32[32]{0:T(128)} %vm_s.1, f32[32]{0:T(128)} %vp_s.1, f32[32]{0:T(128)} %vs_s.1, f32[32]{0:T(128)} %op_s.1, f32[32]{0:T(128)} %pr_s.3, s32[3,1,8]{2,1,0:T(1,128)} %bitcast.4, bf16[8,512]{1,0:T(8,128)(2,1)} %lv.1, ...), custom_call_target="tpu_custom_call" | custom-call | tf_op jit(solution)/shard_map/pallas_call | solution.py:758
  72.6 3.7 %shard_map.167 = (bf16[8,512,256]{2,1,0:T(8,128)(2,1)}, bf16[8,512]{1,0:T(8,128)(2,1)}, f32[1,8]{1,0:T(1,128)}) custom-call(s32[32]{0:T(128)} %anc.3, s32[8]{0:T(128)} %get-tuple-element.10.pos, f32[32]{0:T(128)} %pr_s.3, bf16[8,512,256]{2,1,0:T(8,128)(2,1)} %get-tuple-element.11.res, f32[8,512]{1,0:T(8,128)} %get-tuple-element.12.vol, ...), custom_call_target="tpu_custom_call" | custom-call | tf_op jit(solution)/shard_map/pallas_call | solution.py:796

commit v4 on v3

--- a/solution.py
+++ b/solution.py
@@ -274,8 +274,8 @@
 
         return 0
 
+    lax.fori_loop(0, 2, start_copy, 0)
     lax.fori_loop(0, 4, start_mat, 0)
-    lax.fori_loop(0, 2, start_copy, 0)
     lax.fori_loop(4, 2 * KEEP, fill, 0)
 
     def start_more(r, _):
@@ -538,16 +538,22 @@
         @pl.when(kind == BUILD)
         def _():
             for n in pair:
-                pass_two(n)
-            for n in pair:
-                pass_on(n + 2)
-            for n in pair:
                 arrive(n)
             for n in pair:
                 build(n)
             draw(pair, 0, [cT[n] for n in pair])
             for n in pair:
                 send_halo(n, 0)
+
+            @pl.when(r == 0)
+            def _():
+                for n in pair:
+                    pass_on(n)
+
+            for n in pair:
+                pass_two(n)
+            for n in pair:
+                pass_on(n + 2)
 
         @pl.when(kind == SERVE)
         def _():
@@ -637,8 +643,6 @@
             send_vol(d).wait_recv()
 
     ask()
-    pass_on(0)
-    pass_on(1)
     lax.fori_loop(0, len(ORDER), task, 0)
 
     def join(buf, here):

time: 76.7 us -> 76.7 us (level)
  no operation moved by 1% of the time
where the time goes in v4:
time: 76.7 us; the launch traced here: 76.1 us
  Pallas kernels  75.5 us (98%)
    pallas_call x1, Pallas kernels, local(): pl.pallas_call(kernel, out_shape=(jax.ShapeDtypeStruct((PD, SD, K), BF16)...  71.8 us
    pallas_call x1, Pallas kernels, local(): pl.pallas_call(reorder, out_shape=(jax.ShapeDtypeStruct((PD, SD, K), BF16...  3.73 us

profile of v4, /device:TPU:1, one launch (start us, length us, event | category | flops | bytes accessed | tf_op | source)
XLA Modules:
  0.0 76.1 jit_solution(16671039984137283194)
XLA Ops:
  0.6 71.8 %shard_map.166 = (bf16[8,512,256]{2,1,0:T(8,128)(2,1)}, f32[8,512]{1,0:T(8,128)}, f32[8,128]{1,0:T(8,128)}, s32[8]{0:T(128)}) custom-call(s32[32]{0:T(128)} %anc.3, f32[32]{0:T(128)} %vm_s.1, f32[32]{0:T(128)} %vp_s.1, f32[32]{0:T(128)} %vs_s.1, f32[32]{0:T(128)} %op_s.1, f32[32]{0:T(128)} %pr_s.3, s32[3,1,8]{2,1,0:T(1,128)} %bitcast.4, bf16[8,512]{1,0:T(8,128)(2,1)} %lv.1, ...), custom_call_target="tpu_custom_call" | custom-call | tf_op jit(solution)/shard_map/pallas_call | solution.py:762
  72.4 3.7 %shard_map.167 = (bf16[8,512,256]{2,1,0:T(8,128)(2,1)}, bf16[8,512]{1,0:T(8,128)(2,1)}, f32[1,8]{1,0:T(1,128)}) custom-call(s32[32]{0:T(128)} %anc.3, s32[8]{0:T(128)} %get-tuple-element.10.pos, f32[32]{0:T(128)} %pr_s.3, bf16[8,512,256]{2,1,0:T(8,128)(2,1)} %get-tuple-element.11.res, f32[8,512]{1,0:T(8,128)} %get-tuple-element.12.vol, ...), custom_call_target="tpu_custom_call" | custom-call | tf_op jit(solution)/shard_map/pallas_call | solution.py:800
